TPU v7x, 32 devices: a whole 2x2x4 slice. The times are simulated.
32 devices in a mesh: section: 2 (over y), tensor: 4 (over z), ctx: 4 (over x, core).
Axes of the slice: x: 2, y: 2, z: 4, core: 2. Of those that a mesh axis runs over, the one named last changes fastest.
Arguments:
- latents: bfloat16 [3, 1024, 1152], P(None, 'ctx'), may hold values from -6 to 6
- condition: float32 [3, 1152], P(None, 'ctx'), may hold values from -6 to 6
- cotangent: bfloat16 [3, 1024, 1152], P(None, 'ctx'), may hold values from -6 to 6
- w_ada: bfloat16 [2, 1152, 6912], P('section', 'ctx', 'tensor'), may hold values from -0.1875 to 0.1875
- b_ada: float32 [2, 6912], P('section', 'tensor'), may hold values from -3 to 3
- w_qkv: bfloat16 [2, 1152, 3, 1152], P('section', None, None, 'tensor'), may hold values from -0.1875 to 0.1875
- b_qv: float32 [2, 2, 1152], P('section', None, 'tensor'), may hold values from -3 to 3
- w_out: bfloat16 [2, 1152, 1152], P('section', 'tensor'), may hold values from -1.5 to 1.5
- b_out: float32 [2, 1152], P('section'), may hold values from -3 to 3
- w_fc1: bfloat16 [2, 1152, 4608], P('section', None, 'tensor'), may hold values from -0.1875 to 0.1875
- b_fc1: float32 [2, 4608], P('section', 'tensor'), may hold values from -3 to 3
- w_fc2: bfloat16 [2, 4608, 1152], P('section', 'tensor'), may hold values from -0.09375 to 0.09375
- b_fc2: float32 [2, 1152], P('section'), may hold values from -3 to 3
Outputs:
- block_out: bfloat16 [2, 3, 1024, 1152], P('section', None, 'ctx')
- in_grad: float32 [2, 3, 1024, 1152], P('section', None, 'ctx')
- cond_grad: float32 [3, 1152], P(None, 'ctx')
- grad_w_ada: float32 [2, 1152, 6912], P('section', 'ctx', 'tensor')
- grad_b_ada: float32 [2, 6912], P('section', 'tensor')
- grad_w_qkv: float32 [2, 1152, 3, 1152], P('section', 'ctx', None, 'tensor')
- grad_b_qv: float32 [2, 2, 1152], P('section', None, 'tensor')
- grad_w_out: float32 [2, 1152, 1152], P('section', 'tensor', 'ctx')
- grad_b_out: float32 [2, 1152], P('section')
- grad_w_fc1: float32 [2, 1152, 4608], P('section', 'ctx', 'tensor')
- grad_b_fc1: float32 [2, 4608], P('section', 'tensor')
- grad_w_fc2: float32 [2, 4608, 1152], P('section', 'tensor', 'ctx')
- grad_b_fc2: float32 [2, 1152], P('section')
All inputs are finite; a program needn't handle non-finite values.
Results may differ from a plain program's by a relative error of at most 0.025.
Values may be sent and summed in bfloat16 or wider, within the bound.
A program may use at most 192 MiB of HBM per device.

v0:
```python
import math

import jax
import jax.numpy as jnp
from jax import lax
from jax.sharding import PartitionSpec as P

HD = 72
MB = 1
NMB = 3


EPSILON = 1e-06


def passed_along(shard, axis, by):
    devices = lax.axis_size(axis)
    pairs = [(i, i + by) for i in range(devices) if 0 <= i + by < devices]
    return lax.ppermute(shard, axis, pairs)


def layer_norm(values):
    centre = jnp.mean(values, axis=-1, keepdims=True)
    centred = values - centre
    variance = jnp.mean(centred * centred, axis=-1, keepdims=True)
    inverse = lax.rsqrt(variance + EPSILON)
    return (centred * inverse, inverse)


def norm_back(normed, inverse, upstream):
    mean_grad = jnp.mean(upstream, axis=-1, keepdims=True)
    mean_cross = jnp.mean(upstream * normed, axis=-1, keepdims=True)
    return inverse * (upstream - mean_grad - normed * mean_cross)


def gelu_back(pre_act, upstream):
    unused_out, pullback = jax.vjp(
        lambda pre_value: jax.nn.gelu(pre_value, approximate=True), pre_act
    )
    return pullback(upstream)[0]


def head_view(array):
    return array.reshape(array.shape[0], array.shape[1], array.shape[2] // HD, HD)


def attend(queries, keys_all, values_all):
    softmax_scale = 1.0 / math.sqrt(HD)
    scores = (
        jnp.einsum(
            "bqhd,bkhd->bhqk",
            head_view(queries),
            head_view(keys_all),
            preferred_element_type=jnp.float32,
        )
        * softmax_scale
    )
    row_peak = jnp.max(scores, axis=-1, keepdims=True)
    log_total = row_peak + jnp.log(jnp.sum(jnp.exp(scores - row_peak), axis=-1, keepdims=True))
    prob_bf = jnp.exp(scores - log_total).astype(jnp.bfloat16)
    context = jnp.einsum(
        "bhqk,bkhd->bqhd", prob_bf, head_view(values_all), preferred_element_type=jnp.float32
    )
    return (context.astype(jnp.bfloat16).reshape(queries.shape), log_total)


def row_delta(context, context_grad):
    delta_rows = jnp.sum(
        head_view(context_grad).astype(jnp.float32) * head_view(context).astype(jnp.float32),
        axis=-1,
    )
    return jnp.transpose(delta_rows, (0, 2, 1))[..., None]


def score_terms(query_heads, key_heads, value_heads, grad_heads, log_total, delta_rows):
    softmax_scale = 1.0 / math.sqrt(HD)
    scores = (
        jnp.einsum("bqhd,bkhd->bhqk", query_heads, key_heads, preferred_element_type=jnp.float32)
        * softmax_scale
    )
    prob_full = jnp.exp(scores - log_total)
    prob_grad = jnp.einsum(
        "bqhd,bkhd->bhqk", grad_heads, value_heads, preferred_element_type=jnp.float32
    )
    score_grad = (prob_full * (prob_grad - delta_rows)).astype(jnp.bfloat16)
    return (prob_full, score_grad)


def key_side(query_heads, grad_heads, prob_full, score_grad, key_shape):
    softmax_scale = 1.0 / math.sqrt(HD)
    prob_bf = prob_full.astype(jnp.bfloat16)
    key_part = (
        jnp.einsum("bhqk,bqhd->bkhd", score_grad, query_heads, preferred_element_type=jnp.float32)
        * softmax_scale
    )
    value_part = jnp.einsum(
        "bhqk,bqhd->bkhd", prob_bf, grad_heads, preferred_element_type=jnp.float32
    )
    return (key_part.reshape(key_shape), value_part.reshape(key_shape))


def attention_grads(queries, keys_all, values_all, log_total, context, context_grad):
    softmax_scale = 1.0 / math.sqrt(HD)
    query_heads = head_view(queries)
    key_heads = head_view(keys_all)
    grad_heads = head_view(context_grad)
    delta_rows = row_delta(context, context_grad)
    prob_full, score_grad = score_terms(
        query_heads, key_heads, head_view(values_all), grad_heads, log_total, delta_rows
    )
    query_grad = (
        jnp.einsum("bhqk,bkhd->bqhd", score_grad, key_heads, preferred_element_type=jnp.float32)
        * softmax_scale
    ).reshape(queries.shape)
    key_part, value_part = key_side(query_heads, grad_heads, prob_full, score_grad, keys_all.shape)
    key_grad, value_grad = (
        lax.psum_scatter(
            key_part.astype(jnp.bfloat16), "ctx", scatter_dimension=1, tiled=True
        ).astype(jnp.float32),
        lax.psum_scatter(
            value_part.astype(jnp.bfloat16), "ctx", scatter_dimension=1, tiled=True
        ).astype(jnp.float32),
    )
    return (query_grad, key_grad, value_grad)


def forward_block(block_in, mod_rows, weights):
    w_qkv, b_qv, w_out, b_out, w_fc1, b_fc1, w_fc2, b_fc2 = weights
    latent_count, token_count, model_width = block_in.shape
    row_count = latent_count * token_count
    local_cols = w_qkv.shape[-1]
    residual = block_in.astype(jnp.float32)
    normed_a, inverse_a = layer_norm(residual)
    attn_in = (normed_a * (1.0 + mod_rows[:, 1, None, :]) + mod_rows[:, 0, None, :]).astype(
        jnp.bfloat16
    )
    projected = jnp.dot(
        attn_in.reshape(row_count, model_width),
        w_qkv.reshape(model_width, 3 * local_cols),
        preferred_element_type=jnp.float32,
    ).reshape(latent_count, token_count, 3, local_cols)
    queries = (projected[:, :, 0] + b_qv[0]).astype(jnp.bfloat16)
    key_rows = projected[:, :, 1].astype(jnp.bfloat16)
    values = (projected[:, :, 2] + b_qv[1]).astype(jnp.bfloat16)
    keys_all, values_all = (
        lax.all_gather(key_rows, "ctx", axis=1, tiled=True),
        lax.all_gather(values, "ctx", axis=1, tiled=True),
    )
    context, log_total = attend(queries, keys_all, values_all)
    attn_term = jnp.dot(
        context.reshape(row_count, local_cols), w_out, preferred_element_type=jnp.float32
    )
    attn_out = (
        lax.psum(attn_term.astype(jnp.bfloat16), "tensor")
        .astype(jnp.float32)
        .reshape(block_in.shape)
        + b_out
    )
    middle = residual + mod_rows[:, 2, None, :] * attn_out
    normed_m, inverse_m = layer_norm(middle)
    mlp_in = (normed_m * (1.0 + mod_rows[:, 4, None, :]) + mod_rows[:, 3, None, :]).astype(
        jnp.bfloat16
    )
    pre_act = (
        jnp.dot(mlp_in.reshape(row_count, model_width), w_fc1, preferred_element_type=jnp.float32)
        + b_fc1
    )
    hidden = jax.nn.gelu(pre_act, approximate=True).astype(jnp.bfloat16)
    mlp_term = jnp.dot(hidden, w_fc2, preferred_element_type=jnp.float32)
    mlp_out = (
        lax.psum(mlp_term.astype(jnp.bfloat16), "tensor")
        .astype(jnp.float32)
        .reshape(block_in.shape)
        + b_fc2
    )
    block_res = (middle + mod_rows[:, 5, None, :] * mlp_out).astype(jnp.bfloat16)
    stored = (
        normed_a,
        inverse_a,
        attn_in,
        queries,
        keys_all,
        values_all,
        log_total,
        context,
        attn_out,
        normed_m,
        inverse_m,
        mlp_in,
        pre_act,
        hidden,
        mlp_out,
    )
    return (block_res, stored)


def backward_block(upstream, stored, mod_rows, weights):
    w_qkv, b_qv, w_out, b_out, w_fc1, b_fc1, w_fc2, b_fc2 = weights
    (
        normed_a,
        inverse_a,
        attn_in,
        queries,
        keys_all,
        values_all,
        log_total,
        context,
        attn_out,
        normed_m,
        inverse_m,
        mlp_in,
        pre_act,
        hidden,
        mlp_out,
    ) = stored
    latent_count, token_count, model_width = upstream.shape
    row_count = latent_count * token_count
    local_cols = queries.shape[-1]
    gate_m_grad = jnp.sum(upstream * mlp_out, axis=1)
    mlp_grad = upstream * mod_rows[:, 5, None, :]
    mlp_grad_b = mlp_grad.reshape(row_count, model_width).astype(jnp.bfloat16)
    grad_w2 = jnp.dot(hidden.T, mlp_grad_b, preferred_element_type=jnp.float32)
    grad_b2 = jnp.sum(mlp_grad, axis=(0, 1))
    pre_grad = gelu_back(pre_act, jnp.dot(mlp_grad_b, w_fc2.T, preferred_element_type=jnp.float32))
    pre_grad_b = pre_grad.astype(jnp.bfloat16)
    grad_w1 = jnp.dot(
        mlp_in.reshape(row_count, model_width).T, pre_grad_b, preferred_element_type=jnp.float32
    )
    grad_b1 = jnp.sum(pre_grad, axis=0)
    mlp_in_grad = (
        lax.psum(
            jnp.dot(pre_grad_b, w_fc1.T, preferred_element_type=jnp.float32).astype(jnp.bfloat16),
            "tensor",
        )
        .astype(jnp.float32)
        .reshape(upstream.shape)
    )
    shift_m_grad = jnp.sum(mlp_in_grad, axis=1)
    scale_m_grad = jnp.sum(mlp_in_grad * normed_m, axis=1)
    middle_grad = upstream + norm_back(
        normed_m, inverse_m, mlp_in_grad * (1.0 + mod_rows[:, 4, None, :])
    )
    gate_a_grad = jnp.sum(middle_grad * attn_out, axis=1)
    attn_grad = middle_grad * mod_rows[:, 2, None, :]
    attn_grad_b = attn_grad.reshape(row_count, model_width).astype(jnp.bfloat16)
    grad_wo = jnp.dot(
        context.reshape(row_count, local_cols).T, attn_grad_b, preferred_element_type=jnp.float32
    )
    grad_bo = jnp.sum(attn_grad, axis=(0, 1))
    context_grad = (
        jnp.dot(attn_grad_b, w_out.T, preferred_element_type=jnp.float32)
        .astype(jnp.bfloat16)
        .reshape(queries.shape)
    )
    query_grad, key_grad, value_grad = attention_grads(
        queries, keys_all, values_all, log_total, context, context_grad
    )
    grad_bqv = jnp.stack([jnp.sum(query_grad, axis=(0, 1)), jnp.sum(value_grad, axis=(0, 1))])
    qkv_grad_b = (
        jnp.stack([query_grad, key_grad, value_grad], axis=2)
        .astype(jnp.bfloat16)
        .reshape(row_count, 3 * local_cols)
    )
    grad_wqkv = jnp.dot(
        attn_in.reshape(row_count, model_width).T, qkv_grad_b, preferred_element_type=jnp.float32
    ).reshape(model_width, 3, local_cols)
    attn_in_grad = (
        lax.psum(
            jnp.dot(
                qkv_grad_b,
                w_qkv.reshape(model_width, 3 * local_cols).T,
                preferred_element_type=jnp.float32,
            ).astype(jnp.bfloat16),
            "tensor",
        )
        .astype(jnp.float32)
        .reshape(upstream.shape)
    )
    shift_a_grad = jnp.sum(attn_in_grad, axis=1)
    scale_a_grad = jnp.sum(attn_in_grad * normed_a, axis=1)
    input_grad = middle_grad + norm_back(
        normed_a, inverse_a, attn_in_grad * (1.0 + mod_rows[:, 1, None, :])
    )
    mod_grad = jnp.stack(
        [shift_a_grad, scale_a_grad, gate_a_grad, shift_m_grad, scale_m_grad, gate_m_grad], axis=1
    )
    return (
        input_grad,
        mod_grad,
        (grad_wqkv, grad_bqv, grad_wo, grad_bo, grad_w1, grad_b1, grad_w2, grad_b2),
    )


def local(
    latents,
    condition,
    cotangent,
    w_ada,
    b_ada,
    w_qkv,
    b_qv,
    w_out,
    b_out,
    w_fc1,
    b_fc1,
    w_fc2,
    b_fc2,
):
    weights = (w_qkv[0], b_qv[0], w_out[0], b_out[0], w_fc1[0], b_fc1[0], w_fc2[0], b_fc2[0])
    section_index = lax.axis_index("section")
    latent_total, token_count, model_width = latents.shape
    width_cols = b_ada.shape[-1]
    col_offset = lax.axis_index("tensor") * width_cols
    cond_act = jax.nn.silu(condition).astype(jnp.bfloat16)
    mod_part = jnp.dot(cond_act, w_ada[0], preferred_element_type=jnp.float32)
    mod_local = lax.psum(mod_part, "ctx") + b_ada[0]
    modulation = lax.all_gather(mod_local, "tensor", axis=1, tiled=True).reshape(
        latent_total, 6, model_width
    )
    received = jnp.zeros((MB, token_count, model_width), jnp.bfloat16)
    block_out = jnp.zeros_like(latents)
    kept_states = []
    for forward_tick in range(NMB + 1):
        micro_index = forward_tick - section_index
        is_valid = (micro_index >= 0) & (micro_index < NMB)
        offset = jnp.clip(micro_index, 0, NMB - 1) * MB
        own_rows = lax.dynamic_slice_in_dim(latents, offset, MB, 0)
        block_in = jnp.where(section_index == 0, own_rows, received)
        mod_rows = lax.dynamic_slice_in_dim(modulation, offset, MB, 0)
        block_res, stored = forward_block(block_in, mod_rows, weights)
        kept_states.append(stored)
        previous = lax.dynamic_slice_in_dim(block_out, offset, MB, 0)
        block_out = lax.dynamic_update_slice_in_dim(
            block_out, jnp.where(is_valid, block_res, previous), offset, 0
        )
        if forward_tick < NMB:
            received = passed_along(block_res, "section", 1)
    in_grads = jnp.zeros(latents.shape, jnp.float32)
    mod_grads = jnp.zeros((latent_total, width_cols), jnp.float32)
    big_local = tuple(
        (
            jnp.zeros(weight.shape, jnp.float32)
            for weight in (weights[0], weights[2], weights[4], weights[6])
        )
    )
    small_local = tuple(
        (
            jnp.zeros(weight.shape, jnp.float32)
            for weight in (weights[1], weights[3], weights[5], weights[7])
        )
    )
    shares = None
    grad_received = jnp.zeros((MB, token_count, model_width), jnp.float32)
    for back_tick in range(NMB + 1):
        forward_tick = NMB - back_tick
        micro_index = forward_tick - section_index
        is_valid = (micro_index >= 0) & (micro_index < NMB)
        offset = jnp.clip(micro_index, 0, NMB - 1) * MB
        own_cot = lax.dynamic_slice_in_dim(cotangent, offset, MB, 0).astype(jnp.float32)
        upstream = jnp.where(section_index == 1, own_cot, grad_received)
        mod_rows = lax.dynamic_slice_in_dim(modulation, offset, MB, 0)
        stored = kept_states[forward_tick]
        input_grad, mod_grad, grad_terms = backward_block(upstream, stored, mod_rows, weights)
        masked = tuple((jnp.where(is_valid, term, 0.0) for term in grad_terms))
        previous = lax.dynamic_slice_in_dim(in_grads, offset, MB, 0)
        in_grads = lax.dynamic_update_slice_in_dim(
            in_grads, jnp.where(is_valid, input_grad, previous), offset, 0
        )
        mod_piece = lax.dynamic_slice_in_dim(
            mod_grad.reshape(MB, 6 * model_width), col_offset, width_cols, 1
        )
        prior = lax.dynamic_slice_in_dim(mod_grads, offset, MB, 0)
        mod_grads = lax.dynamic_update_slice_in_dim(
            mod_grads, jnp.where(is_valid, mod_piece, prior), offset, 0
        )
        small_local = (
            small_local[0] + masked[1],
            small_local[1] + masked[3],
            small_local[2] + masked[5],
            small_local[3] + masked[7],
        )
        big_local = (
            big_local[0] + masked[0],
            big_local[1] + masked[2],
            big_local[2] + masked[4],
            big_local[3] + masked[6],
        )
        if back_tick < NMB:
            grad_received = passed_along(input_grad.astype(jnp.bfloat16), "section", -1).astype(
                input_grad.dtype
            )
    shares = (
        lax.psum_scatter(
            big_local[0].astype(jnp.bfloat16), "ctx", scatter_dimension=0, tiled=True
        ).astype(jnp.float32),
        lax.psum_scatter(
            big_local[1].astype(jnp.bfloat16), "ctx", scatter_dimension=1, tiled=True
        ).astype(jnp.float32),
        lax.psum_scatter(
            big_local[2].astype(jnp.bfloat16), "ctx", scatter_dimension=0, tiled=True
        ).astype(jnp.float32),
        lax.psum_scatter(
            big_local[3].astype(jnp.bfloat16), "ctx", scatter_dimension=1, tiled=True
        ).astype(jnp.float32),
    )
    small_sums = lax.psum(
        (mod_grads, small_local[0], small_local[1], small_local[2], small_local[3]), "ctx"
    )
    mod_total = small_sums[0]
    mod_rounded = mod_total.astype(jnp.bfloat16)
    grad_w_ada = jnp.dot(cond_act.T, mod_rounded, preferred_element_type=jnp.float32)[None]
    grad_b_ada = jnp.sum(mod_total, axis=0)[None]
    cond_part = jnp.dot(mod_rounded, w_ada[0].T, preferred_element_type=jnp.float32)
    cond_sum = lax.psum(cond_part, ("section", "tensor"))
    sigmoid_c = jax.nn.sigmoid(condition)
    cond_grad = cond_sum * sigmoid_c * (1.0 + condition * (1.0 - sigmoid_c))
    return (
        block_out[None],
        in_grads[None],
        cond_grad,
        grad_w_ada,
        grad_b_ada,
        shares[0][None],
        small_sums[1][None],
        shares[1][None],
        small_sums[2][None],
        shares[2][None],
        small_sums[3][None],
        shares[3][None],
        small_sums[4][None],
    )


def solution(mesh):
    return jax.shard_map(
        local,
        mesh=mesh,
        in_specs=(
            P(None, "ctx", None),
            P(None, "ctx"),
            P(None, "ctx", None),
            P("section", "ctx", "tensor"),
            P("section", "tensor"),
            P("section", None, None, "tensor"),
            P("section", None, "tensor"),
            P("section", "tensor", None),
            P("section", None),
            P("section", None, "tensor"),
            P("section", "tensor"),
            P("section", "tensor", None),
            P("section", None),
        ),
        out_specs=(
            P("section", None, "ctx", None),
            P("section", None, "ctx", None),
            P(None, "ctx"),
            P("section", "ctx", "tensor"),
            P("section", "tensor"),
            P("section", "ctx", None, "tensor"),
            P("section", None, "tensor"),
            P("section", "tensor", "ctx"),
            P("section", None),
            P("section", "ctx", "tensor"),
            P("section", "tensor"),
            P("section", "tensor", "ctx"),
            P("section", None),
        ),
        check_vma=False,
    )
```

profile of v0, /device:TPU:0, one launch (start us, length us, event | category | flops | bytes accessed | tf_op | source)
XLA Modules:
  0.0 1312.8 jit_solution(15437417697808254433)
XLA Ops:
  8.9 12.9 psum.161
  22.5 13.6 %all-gather.4 = f32[4,1728,3]{1,2,0:T(4,128)S(1)} all-gather(f32[1,1728,3]{1,2,0:T(4,128)S(1)} %add_bitcast_fusion), channel_id=1, replica_groups=mesh['section'=2,'tensor'=4,'ctx'=4] {'tensor'}, dimensions={0}, use_global_device_ids=true | all-gather | bytes 103680 | tf_op jit(solution)/shard_map/all_gather | solution.py:317
  66.2 40.0 %all-reduce.18.cloned.1.call-done = bf16[256,1152]{1,0:T(8,128)(2,1)} async-done(((bf16[256,1152]{1,0:T(8,128)(2,1)}), bf16[256,1152]{1,0:T(8,128)(2,1)}) %all-reduce.18.cloned.1.call-update) | async-done | bytes 589840 | tf_op jit(solution)/shard_map/psum | solution.py:154
  116.9 37.9 %all-reduce.20.cloned.1.call-done = bf16[256,1152]{1,0:T(8,128)(2,1)} async-done(((bf16[256,1152]{1,0:T(8,128)(2,1)}), bf16[256,1152]{1,0:T(8,128)(2,1)}) %all-reduce.20.cloned.1.call-update) | async-done | bytes 589840 | tf_op jit(solution)/shard_map/psum | solution.py:171
  162.6 11.9 collective-permute-done
  196.5 38.7 %all-reduce.22.cloned.1.call-done = bf16[256,1152]{1,0:T(8,128)(2,1)} async-done(((bf16[256,1152]{1,0:T(8,128)(2,1)}), bf16[256,1152]{1,0:T(8,128)(2,1)}) %all-reduce.22.cloned.1.call-update) | async-done | bytes 589840 | tf_op jit(solution)/shard_map/psum | solution.py:154
  243.0 39.3 %all-reduce.24.cloned.1.call-done = bf16[256,1152]{1,0:T(8,128)(2,1)} async-done(((bf16[256,1152]{1,0:T(8,128)(2,1)}), bf16[256,1152]{1,0:T(8,128)(2,1)}) %all-reduce.24.cloned.1.call-update) | async-done | bytes 589840 | tf_op jit(solution)/shard_map/psum | solution.py:171
  288.5 11.9 collective-permute-done.1
  323.8 38.3 %all-reduce.26.cloned.1.call-done = bf16[256,1152]{1,0:T(8,128)(2,1)} async-done(((bf16[256,1152]{1,0:T(8,128)(2,1)}), bf16[256,1152]{1,0:T(8,128)(2,1)}) %all-reduce.26.cloned.1.call-update) | async-done | bytes 589840 | tf_op jit(solution)/shard_map/psum | solution.py:154
  370.1 39.3 %all-reduce.28.cloned.1.call-done = bf16[256,1152]{1,0:T(8,128)(2,1)} async-done(((bf16[256,1152]{1,0:T(8,128)(2,1)}), bf16[256,1152]{1,0:T(8,128)(2,1)}) %all-reduce.28.cloned.1.call-update) | async-done | bytes 589840 | tf_op jit(solution)/shard_map/psum | solution.py:171
  450.8 38.5 %all-reduce.30.cloned.1.call-done = bf16[256,1152]{1,0:T(8,128)(2,1)} async-done(((bf16[256,1152]{1,0:T(8,128)(2,1)}), bf16[256,1152]{1,0:T(8,128)(2,1)}) %all-reduce.30.cloned.1.call-update) | async-done | bytes 589840 | tf_op jit(solution)/shard_map/psum | solution.py:154
  500.7 39.2 %all-reduce.32.cloned.1.call-done = bf16[256,1152]{1,0:T(8,128)(2,1)} async-done(((bf16[256,1152]{1,0:T(8,128)(2,1)}), bf16[256,1152]{1,0:T(8,128)(2,1)}) %all-reduce.32.cloned.1.call-update) | async-done | bytes 589840 | tf_op jit(solution)/shard_map/psum | solution.py:231
  558.1 13.7 %reduce-scatter.17.cloned.1.call-done = bf16[1,256,288]{1,2,0:T(8,128)(2,1)} async-done(((bf16[1,1024,288]{1,2,0:T(8,128)(2,1)}), bf16[1,256,288]{1,2,0:T(8,128)(2,1)}) %reduce-scatter.17.cloned.1.call-update) | async-done | bytes 147472 | tf_op jit(solution)/shard_map/reduce_scatter | solution.py:117
  571.8 25.0 %reduce-scatter.19.cloned.1.call-done = bf16[1,256,288]{1,2,0:T(8,128)(2,1)} async-done(((bf16[1,1024,288]{1,2,0:T(8,128)(2,1)}), bf16[1,256,288]{1,2,0:T(8,128)(2,1)}) %reduce-scatter.19.cloned.1.call-update) | async-done | bytes 147472 | tf_op jit(solution)/shard_map/reduce_scatter | solution.py:120
  600.4 39.8 %all-reduce.34.cloned.1.call-done = bf16[256,1152]{1,0:T(8,128)(2,1)} async-done(((bf16[256,1152]{1,0:T(8,128)(2,1)}), bf16[256,1152]{1,0:T(8,128)(2,1)}) %all-reduce.34.cloned.1.call-update) | async-done | bytes 589840 | tf_op jit(solution)/shard_map/psum | solution.py:268
  650.2 14.8 %collective-permute-done.3 = bf16[1,256,1152]{2,1,0:T(8,128)(2,1)S(1)} collective-permute-done((bf16[1,256,1152]{2,1,0:T(8,128)(2,1)S(1)}, bf16[1,256,1152]{2,1,0:T(8,128)(2,1)S(1)}, u32[]{:S(2)}, u32[]{:S(2)}) %collective-permute-start.3) | collective-permute-done | bytes 589856 | tf_op jit(solution)/shard_map/ppermute | solution.py:19
  671.0 37.6 %all-reduce.36.cloned.1.call-done = bf16[256,1152]{1,0:T(8,128)(2,1)} async-done(((bf16[256,1152]{1,0:T(8,128)(2,1)}), bf16[256,1152]{1,0:T(8,128)(2,1)}) %all-reduce.36.cloned.1.call-update) | async-done | bytes 589840 | tf_op jit(solution)/shard_map/psum | solution.py:231
  728.8 13.7 %reduce-scatter.21.cloned.1.call-done = bf16[1,256,288]{1,2,0:T(8,128)(2,1)} async-done(((bf16[1,1024,288]{1,2,0:T(8,128)(2,1)}), bf16[1,256,288]{1,2,0:T(8,128)(2,1)}) %reduce-scatter.21.cloned.1.call-update) | async-done | bytes 147472 | tf_op jit(solution)/shard_map/reduce_scatter | solution.py:117
  742.5 24.4 %reduce-scatter.23.cloned.1.call-done = bf16[1,256,288]{1,2,0:T(8,128)(2,1)} async-done(((bf16[1,1024,288]{1,2,0:T(8,128)(2,1)}), bf16[1,256,288]{1,2,0:T(8,128)(2,1)}) %reduce-scatter.23.cloned.1.call-update) | async-done | bytes 147472 | tf_op jit(solution)/shard_map/reduce_scatter | solution.py:120
  770.5 39.8 %all-reduce.38.cloned.1.call-done = bf16[256,1152]{1,0:T(8,128)(2,1)} async-done(((bf16[256,1152]{1,0:T(8,128)(2,1)}), bf16[256,1152]{1,0:T(8,128)(2,1)}) %all-reduce.38.cloned.1.call-update) | async-done | bytes 589840 | tf_op jit(solution)/shard_map/psum | solution.py:268
  819.5 15.0 %collective-permute-done.4 = bf16[1,256,1152]{2,1,0:T(8,128)(2,1)S(1)} collective-permute-done((bf16[1,256,1152]{2,1,0:T(8,128)(2,1)S(1)}, bf16[1,256,1152]{2,1,0:T(8,128)(2,1)S(1)}, u32[]{:S(2)}, u32[]{:S(2)}) %collective-permute-start.4) | collective-permute-done | bytes 589856 | tf_op jit(solution)/shard_map/ppermute | solution.py:19
  840.9 37.1 %all-reduce.40.cloned.1.call-done = bf16[256,1152]{1,0:T(8,128)(2,1)} async-done(((bf16[256,1152]{1,0:T(8,128)(2,1)}), bf16[256,1152]{1,0:T(8,128)(2,1)}) %all-reduce.40.cloned.1.call-update) | async-done | bytes 589840 | tf_op jit(solution)/shard_map/psum | solution.py:231
  898.0 13.8 %reduce-scatter.25.cloned.1.call-done = bf16[1,256,288]{1,2,0:T(8,128)(2,1)} async-done(((bf16[1,1024,288]{1,2,0:T(8,128)(2,1)}), bf16[1,256,288]{1,2,0:T(8,128)(2,1)}) %reduce-scatter.25.cloned.1.call-update) | async-done | bytes 147472 | tf_op jit(solution)/shard_map/reduce_scatter | solution.py:117
  911.8 24.4 %reduce-scatter.27.cloned.1.call-done = bf16[1,256,288]{1,2,0:T(8,128)(2,1)} async-done(((bf16[1,1024,288]{1,2,0:T(8,128)(2,1)}), bf16[1,256,288]{1,2,0:T(8,128)(2,1)}) %reduce-scatter.27.cloned.1.call-update) | async-done | bytes 147472 | tf_op jit(solution)/shard_map/reduce_scatter | solution.py:120
  939.8 39.8 %all-reduce.42.cloned.1.call-done = bf16[256,1152]{1,0:T(8,128)(2,1)} async-done(((bf16[256,1152]{1,0:T(8,128)(2,1)}), bf16[256,1152]{1,0:T(8,128)(2,1)}) %all-reduce.42.cloned.1.call-update) | async-done | bytes 589840 | tf_op jit(solution)/shard_map/psum | solution.py:268
  988.4 15.0 %collective-permute-done.5 = bf16[1,256,1152]{2,1,0:T(8,128)(2,1)S(1)} collective-permute-done((bf16[1,256,1152]{2,1,0:T(8,128)(2,1)S(1)}, bf16[1,256,1152]{2,1,0:T(8,128)(2,1)S(1)}, u32[]{:S(2)}, u32[]{:S(2)}) %collective-permute-start.5) | collective-permute-done | bytes 589856 | tf_op jit(solution)/shard_map/ppermute | solution.py:19
  1009.6 37.4 %all-reduce.44.cloned.1.call-done = bf16[256,1152]{1,0:T(8,128)(2,1)} async-done(((bf16[256,1152]{1,0:T(8,128)(2,1)}), bf16[256,1152]{1,0:T(8,128)(2,1)}) %all-reduce.44.cloned.1.call-update) | async-done | bytes 589840 | tf_op jit(solution)/shard_map/psum | solution.py:231
  1082.0 24.5 %reduce-scatter.31.cloned.1.call-done = bf16[1,256,288]{1,2,0:T(8,128)(2,1)} async-done(((bf16[1,1024,288]{1,2,0:T(8,128)(2,1)}), bf16[1,256,288]{1,2,0:T(8,128)(2,1)}) %reduce-scatter.31.cloned.1.call-update) | async-done | bytes 147472 | tf_op jit(solution)/shard_map/reduce_scatter | solution.py:120
  1201.9 12.8 all-reduce
  1217.0 20.6 %psum.179 = f32[3,288]{1,0:T(4,128)S(1)} all-reduce(f32[3,288]{1,0:T(4,128)S(1)} %fusion.270), channel_id=1, replica_groups=mesh['section'=2,'tensor'=4,'ctx'=4] {'section','tensor'}, use_global_device_ids=true, to_apply=%region_94.95 | all-reduce | flops 864 | bytes 6912 | tf_op jit(solution)/shard_map/psum | solution.py:414
  1251.6 14.6 %reduce-scatter.35.cloned.1.call-done = bf16[288,1152]{1,0:T(8,128)(2,1)} async-done(((bf16[1152,1152]{1,0:T(8,128)(2,1)}), bf16[288,1152]{1,0:T(8,128)(2,1)}) %reduce-scatter.35.cloned.1.call-update) | async-done | bytes 663568 | tf_op jit(solution)/shard_map/reduce_scatter | solution.py:399
  1268.4 34.8 %reduce-scatter.33.cloned.1.call-done = bf16[288,3,288]{2,0,1:T(8,128)(2,1)} async-done(((bf16[1152,3,288]{2,0,1:T(8,128)(2,1)}), bf16[288,3,288]{2,0,1:T(8,128)(2,1)}) %reduce-scatter.33.cloned.1.call-update) | async-done | bytes 497680 | tf_op jit(solution)/shard_map/reduce_scatter | solution.py:393
  (965 shorter events, 433.9 us)
Async XLA Ops:
  7.2 99.0 %all-reduce.18.cloned.1.call-start = ((), (), s32[]{:S(2)}) async-start(), calls=%async_computation.12 | async-start | bytes 1179648 | tf_op jit(solution)/shard_map/psum | solution.py:154
  65.5 89.2 %all-reduce.20.cloned.1.call-start = ((), (), s32[]{:S(2)}) async-start(), calls=%async_computation.13 | async-start | bytes 1179648 | tf_op jit(solution)/shard_map/psum | solution.py:171
  115.5 119.7 %all-reduce.22.cloned.1.call-start = ((), (), s32[]{:S(2)}) async-start(), calls=%async_computation.14 | async-start | bytes 1179648 | tf_op jit(solution)/shard_map/psum | solution.py:154
  196.5 85.7 %all-reduce.24.cloned.1.call-start = ((), (), s32[]{:S(2)}) async-start(), calls=%async_computation.15 | async-start | bytes 1179648 | tf_op jit(solution)/shard_map/psum | solution.py:171
  242.9 119.1 %all-reduce.26.cloned.1.call-start = ((), (), s32[]{:S(2)}) async-start(), calls=%async_computation.16 | async-start | bytes 1179648 | tf_op jit(solution)/shard_map/psum | solution.py:154
  285.0 15.5 %collective-permute-start.1 = (bf16[1,256,1152]{2,1,0:T(8,128)(2,1)S(1)}, bf16[1,256,1152]{2,1,0:T(8,128)(2,1)S(1)}, u32[]{:S(2)}, u32[]{:S(2)}) collective-permute-start(bf16[1,256,1152]{2,1,0:T(8,128)(2,1)S(1)} %get-tuple-element.157), channel_id=1, source_target_pairs={{0,16},{1,17},{2,18},{3,19},{4,20},{5,21},{6,22},{7,23},{8,24},{9,... | collective-permute-start | bytes 1769480 | tf_op jit(solution)/shard_map/ppermute | solution.py:19
  323.3 86.0 %all-reduce.28.cloned.1.call-start = ((), (), s32[]{:S(2)}) async-start(), calls=%async_computation.17 | async-start | bytes 1179648 | tf_op jit(solution)/shard_map/psum | solution.py:171
  370.0 119.3 %all-reduce.30.cloned.1.call-start = ((), (), s32[]{:S(2)}) async-start(), calls=%async_computation.18 | async-start | bytes 1179648 | tf_op jit(solution)/shard_map/psum | solution.py:154
  412.3 15.5 %collective-permute-start.2 = (bf16[1,256,1152]{2,1,0:T(8,128)(2,1)S(1)}, bf16[1,256,1152]{2,1,0:T(8,128)(2,1)S(1)}, u32[]{:S(2)}, u32[]{:S(2)}) collective-permute-start(bf16[1,256,1152]{2,1,0:T(8,128)(2,1)S(1)} %get-tuple-element.153), channel_id=1, source_target_pairs={{0,16},{1,17},{2,18},{3,19},{4,20},{5,21},{6,22},{7,23},{8,24},{9,... | collective-permute-start | bytes 1769480 | tf_op jit(solution)/shard_map/ppermute | solution.py:19
  450.6 89.3 %all-reduce.32.cloned.1.call-start = ((), (), s32[]{:S(2)}) async-start(), calls=%async_computation.19 | async-start | bytes 1179648 | tf_op jit(solution)/shard_map/psum | solution.py:231
  500.7 71.2 %reduce-scatter.17.cloned.1.call-start = ((), (), s32[]{:S(2)}) async-start(), calls=%async_computation.20 | async-start | bytes 737280 | tf_op jit(solution)/shard_map/reduce_scatter | solution.py:117
  550.2 46.7 %reduce-scatter.19.cloned.1.call-start = ((), (), s32[]{:S(2)}) async-start(), calls=%async_computation.21 | async-start | bytes 737280 | tf_op jit(solution)/shard_map/reduce_scatter | solution.py:120
  554.2 86.0 %all-reduce.34.cloned.1.call-start = ((), (), s32[]{:S(2)}) async-start(), calls=%async_computation.22 | async-start | bytes 1179648 | tf_op jit(solution)/shard_map/psum | solution.py:268
  600.3 108.3 %all-reduce.36.cloned.1.call-start = ((), (), s32[]{:S(2)}) async-start(), calls=%async_computation.23 | async-start | bytes 1179648 | tf_op jit(solution)/shard_map/psum | solution.py:231
  648.5 16.6 %collective-permute-start.3 = (bf16[1,256,1152]{2,1,0:T(8,128)(2,1)S(1)}, bf16[1,256,1152]{2,1,0:T(8,128)(2,1)S(1)}, u32[]{:S(2)}, u32[]{:S(2)}) collective-permute-start(bf16[1,256,1152]{2,1,0:T(8,128)(2,1)S(1)} %get-tuple-element.149), channel_id=1, source_target_pairs={{16,0},{17,1},{18,2},{19,3},{20,4},{21,5},{22,6},{23,7},{24,8},{25... | collective-permute-start | bytes 1769480 | tf_op jit(solution)/shard_map/ppermute | solution.py:19
  671.0 71.5 %reduce-scatter.21.cloned.1.call-start = ((), (), s32[]{:S(2)}) async-start(), calls=%async_computation.24 | async-start | bytes 737280 | tf_op jit(solution)/shard_map/reduce_scatter | solution.py:117
  720.9 46.1 %reduce-scatter.23.cloned.1.call-start = ((), (), s32[]{:S(2)}) async-start(), calls=%async_computation.25 | async-start | bytes 737280 | tf_op jit(solution)/shard_map/reduce_scatter | solution.py:120
  724.9 85.4 %all-reduce.38.cloned.1.call-start = ((), (), s32[]{:S(2)}) async-start(), calls=%async_computation.26 | async-start | bytes 1179648 | tf_op jit(solution)/shard_map/psum | solution.py:268
  770.5 107.6 %all-reduce.40.cloned.1.call-start = ((), (), s32[]{:S(2)}) async-start(), calls=%async_computation.27 | async-start | bytes 1179648 | tf_op jit(solution)/shard_map/psum | solution.py:231
  817.9 16.6 %collective-permute-start.4 = (bf16[1,256,1152]{2,1,0:T(8,128)(2,1)S(1)}, bf16[1,256,1152]{2,1,0:T(8,128)(2,1)S(1)}, u32[]{:S(2)}, u32[]{:S(2)}) collective-permute-start(bf16[1,256,1152]{2,1,0:T(8,128)(2,1)S(1)} %get-tuple-element.147), channel_id=1, source_target_pairs={{16,0},{17,1},{18,2},{19,3},{20,4},{21,5},{22,6},{23,7},{24,8},{25... | collective-permute-start | bytes 1769480 | tf_op jit(solution)/shard_map/ppermute | solution.py:19
  840.5 71.3 %reduce-scatter.25.cloned.1.call-start = ((), (), s32[]{:S(2)}) async-start(), calls=%async_computation.28 | async-start | bytes 737280 | tf_op jit(solution)/shard_map/reduce_scatter | solution.py:117
  890.1 46.1 %reduce-scatter.27.cloned.1.call-start = ((), (), s32[]{:S(2)}) async-start(), calls=%async_computation.29 | async-start | bytes 737280 | tf_op jit(solution)/shard_map/reduce_scatter | solution.py:120
  894.1 85.4 %all-reduce.42.cloned.1.call-start = ((), (), s32[]{:S(2)}) async-start(), calls=%async_computation.30 | async-start | bytes 1179648 | tf_op jit(solution)/shard_map/psum | solution.py:268
  939.7 107.3 %all-reduce.44.cloned.1.call-start = ((), (), s32[]{:S(2)}) async-start(), calls=%async_computation.31 | async-start | bytes 1179648 | tf_op jit(solution)/shard_map/psum | solution.py:231
  986.9 16.6 %collective-permute-start.5 = (bf16[1,256,1152]{2,1,0:T(8,128)(2,1)S(1)}, bf16[1,256,1152]{2,1,0:T(8,128)(2,1)S(1)}, u32[]{:S(2)}, u32[]{:S(2)}) collective-permute-start(bf16[1,256,1152]{2,1,0:T(8,128)(2,1)S(1)} %get-tuple-element.145), channel_id=1, source_target_pairs={{16,0},{17,1},{18,2},{19,3},{20,4},{21,5},{22,6},{23,7},{24,8},{25... | collective-permute-start | bytes 1769480 | tf_op jit(solution)/shard_map/ppermute | solution.py:19
  1009.4 72.6 %reduce-scatter.29.cloned.1.call-start = ((), (), s32[]{:S(2)}) async-start(), calls=%async_computation.32 | async-start | bytes 737280 | tf_op jit(solution)/shard_map/reduce_scatter | solution.py:117
  1060.2 46.2 %reduce-scatter.31.cloned.1.call-start = ((), (), s32[]{:S(2)}) async-start(), calls=%async_computation.33 | async-start | bytes 737280 | tf_op jit(solution)/shard_map/reduce_scatter | solution.py:120
  1064.3 121.6 %reduce-scatter.37.cloned.1.call-start = ((), (), s32[]{:S(2)}) async-start(), calls=%async_computation.36 | async-start | bytes 1105920
  1072.3 120.0 %all-reduce.46.cloned.1.call-start = ((), (), s32[]{:S(2)}) async-start(), calls=%async_computation.38 | async-start | bytes 2359296 | tf_op jit(solution)/shard_map/psum | solution.py:171
  1109.9 135.6 %reduce-scatter.39.cloned.1.call-start = ((), (), s32[]{:S(2)}) async-start(), calls=%async_computation.37 | async-start | bytes 3317760
  1124.7 141.6 %reduce-scatter.35.cloned.1.call-start = ((), (), s32[]{:S(2)}) async-start(), calls=%async_computation.35 | async-start | bytes 3317760 | tf_op jit(solution)/shard_map/reduce_scatter | solution.py:399
  1134.8 168.5 %reduce-scatter.33.cloned.1.call-start = ((), (), s32[]{:S(2)}) async-start(), calls=%async_computation.34 | async-start | bytes 3317760 | tf_op jit(solution)/shard_map/reduce_scatter | solution.py:393
  (316 other events, 1529.9 us)
Sparse Core Ops, SparseCore 0:
  65.7 40.5 all-reduce.17
  115.6 39.1 all-reduce.19
  196.6 38.5 all-reduce.21
  243.1 39.1 all-reduce.23
  323.5 38.5 all-reduce.25
  370.1 39.1 all-reduce.27
  450.7 38.5 all-reduce.29
  500.8 39.1 all-reduce.31
  550.3 21.4 reduce-scatter.16
  574.7 22.0 reduce-scatter.18
  600.5 39.6 all-reduce.33
  671.1 37.4 all-reduce.35
  721.0 21.4 reduce-scatter.20
  744.9 22.0 reduce-scatter.22
  770.6 39.6 all-reduce.37
  840.6 37.4 all-reduce.39
  890.2 21.5 reduce-scatter.24
  914.1 22.0 reduce-scatter.26
  939.8 39.6 all-reduce.41
  1009.5 37.4 all-reduce.43
  1060.3 21.4 reduce-scatter.28
  1084.4 22.0 reduce-scatter.30
  1109.6 23.8 reduce-scatter.36
  1136.3 56.0 all-reduce.45
  1194.9 34.1 reduce-scatter.38
  1231.5 34.6 reduce-scatter.34
  1268.6 34.6 reduce-scatter.32
where the time goes:
time: 1320 us; the launch traced here: 1310 us
  waiting for transfers between devices  817 us (62%)
  matrix products  168 us (13%)
  blocking collectives  120 us (9%)
  other arithmetic  104 us (8%)
  local copies, waits for them, and re-layouts  66.8 us (5%)
  between operations  18.8 us (1%)
  starting transfers between devices  18.2 us (1%)
    psum x4, waiting for transfers between devices, forward_block(): lax.psum(attn_term.astype(jnp.bfloat16), 'tensor').astype(jnp.float32)  155 us
    psum x4, waiting for transfers between devices, backward_block(): lax.psum(jnp.dot(pre_grad_b, w_fc1.T, preferred_element_type=jnp.float32)...  151 us
    psum x4, waiting for transfers between devices, forward_block(): lax.psum(mlp_term.astype(jnp.bfloat16), 'tensor').astype(jnp.float32)  121 us
    psum x3, waiting for transfers between devices, backward_block(): lax.psum(jnp.dot(qkv_grad_b, w_qkv.reshape(model_width, 3 * local_cols).T...  119 us
    reduce_scatter x4, waiting for transfers between devices, attention_grads(): lax.psum_scatter(value_part.astype(jnp.bfloat16), 'ctx', scatter_dimensio...  98.3 us
    ppermute x6, waiting for transfers between devices, passed_along(): return lax.ppermute(shard, axis, pairs)  80.6 us
    unnamed x642, local copies, waits for them, and re-layouts  43.1 us
    reduce_scatter x4, waiting for transfers between devices, attention_grads(): lax.psum_scatter(key_part.astype(jnp.bfloat16), 'ctx', scatter_dimension=...  41.2 us
  transfers between devices with their start and end apart: 33, of which 30 were waited for; matrix products, arithmetic and copies ran while one was open for 11% of the time, Pallas kernels for 0%

commit v1 on v0

--- a/solution.py
+++ b/solution.py
@@ -1,8 +1,11 @@
+import functools
 import math
 
 import jax
 import jax.numpy as jnp
 from jax import lax
+from jax.experimental import pallas as pl
+from jax.experimental.pallas import tpu as pltpu
 from jax.sharding import PartitionSpec as P
 
 HD = 72
@@ -11,6 +14,204 @@
 
 
 EPSILON = 1e-06
+
+
+MESH = pl.DeviceIdType.MESH
+PIECES = 2
+
+
+def line_role(d, n, pieces, rows, x_ref, out_ref, acc, buf_l, buf_r, sems):
+    send_r, send_l, recv_l, recv_r, back_send_r, back_send_l, back_recv = sems
+
+    def part(j, s):
+        return pl.ds((j * pieces + s) * rows, rows)
+
+    def hop(src, dst, send_sem, recv_sem, to):
+        return pltpu.make_async_remote_copy(
+            src_ref=src,
+            dst_ref=dst,
+            send_sem=send_sem,
+            recv_sem=recv_sem,
+            device_id={"tensor": to},
+            device_id_type=MESH,
+        )
+
+    def to_right(j, s, src):
+        span = part(j, s)
+        return hop(
+            src.at[span], buf_l.at[span], send_r.at[j, s], recv_l.at[j, s], min(d + 1, n - 1)
+        )
+
+    def to_left(j, s, src):
+        span = part(j, s)
+        return hop(src.at[span], buf_r.at[span], send_l.at[j, s], recv_r.at[j, s], max(d - 1, 0))
+
+    def back_right(j, s):
+        span = part(j, s)
+        return hop(
+            out_ref.at[span],
+            out_ref.at[span],
+            back_send_r.at[j, s],
+            back_recv.at[j, s],
+            min(d + 1, n - 1),
+        )
+
+    def back_left(j, s):
+        span = part(j, s)
+        return hop(
+            out_ref.at[span],
+            out_ref.at[span],
+            back_send_l.at[j, s],
+            back_recv.at[j, s],
+            max(d - 1, 0),
+        )
+
+    def done_at(j, s):
+        return max(
+            2 * j + (n - 1 - j) * pieces + s,
+            2 * (n - 1 - j) + j * pieces + s,
+        )
+
+    steps = []
+    for s in range(pieces):
+        for j in range(d + 1, n):
+            steps.append((2 * d + (n - 1 - j) * pieces + s, 0, j, s))
+            steps.append((done_at(j, s) + 2 * (j - d), 3, j, s))
+        for j in range(d):
+            steps.append((2 * (n - 1 - d) + j * pieces + s, 1, j, s))
+            steps.append((done_at(j, s) + 2 * (d - j), 3, j, s))
+        steps.append((done_at(d, s), 2, d, s))
+    steps.sort()
+    sent = []
+    for when, kind, j, s in steps:
+        span = part(j, s)
+        if kind == 0:
+            src = x_ref
+            if d > 0:
+                to_right(j, s, x_ref).wait_recv()
+                acc[span] = (
+                    x_ref[span].astype(jnp.float32) + buf_l[span].astype(jnp.float32)
+                ).astype(acc.dtype)
+                src = acc
+            sent.append(to_right(j, s, src))
+            sent[-1].start()
+        elif kind == 1:
+            src = x_ref
+            if d < n - 1:
+                to_left(j, s, x_ref).wait_recv()
+                acc[span] = (
+                    x_ref[span].astype(jnp.float32) + buf_r[span].astype(jnp.float32)
+                ).astype(acc.dtype)
+                src = acc
+            sent.append(to_left(j, s, src))
+            sent[-1].start()
+        elif kind == 2:
+            total = x_ref[span].astype(jnp.float32)
+            if d > 0:
+                to_right(j, s, x_ref).wait_recv()
+                total = total + buf_l[span].astype(jnp.float32)
+            if d < n - 1:
+                to_left(j, s, x_ref).wait_recv()
+                total = total + buf_r[span].astype(jnp.float32)
+            out_ref[span] = total.astype(out_ref.dtype)
+            if d < n - 1:
+                sent.append(back_right(j, s))
+                sent[-1].start()
+            if d > 0:
+                sent.append(back_left(j, s))
+                sent[-1].start()
+        else:
+            back_right(j, s).wait_recv()
+            if j < d and d < n - 1:
+                sent.append(back_right(j, s))
+                sent[-1].start()
+            if j > d and d > 0:
+                sent.append(back_left(j, s))
+                sent[-1].start()
+    for copy in sent:
+        copy.wait_send()
+
+
+def line_sum_kernel(n, pieces, rows, x_ref, out_ref, acc, buf_l, buf_r, *sems):
+    me = lax.axis_index("tensor")
+    barrier = pltpu.get_barrier_semaphore()
+    for d in range(n):
+
+        @pl.when(me == d)
+        def role():
+            near = [at for at in (d - 1, d + 1) if 0 <= at < n]
+            for at in near:
+                pl.semaphore_signal(
+                    barrier, inc=1, device_id={"tensor": at}, device_id_type=MESH
+                )
+            pl.semaphore_wait(barrier, len(near))
+            line_role(d, n, pieces, rows, x_ref, out_ref, acc, buf_l, buf_r, sems)
+
+
+def tensor_sum(term):
+    n = lax.axis_size("tensor")
+    if n == 1:
+        return term
+    total_rows, columns = term.shape
+    rows = total_rows // (n * PIECES)
+    sem = pltpu.SemaphoreType.DMA((n, PIECES))
+    return pl.pallas_call(
+        functools.partial(line_sum_kernel, n, PIECES, rows),
+        out_shape=jax.ShapeDtypeStruct(term.shape, term.dtype),
+        in_specs=[pl.BlockSpec(memory_space=pltpu.VMEM)],
+        out_specs=pl.BlockSpec(memory_space=pltpu.VMEM),
+        scratch_shapes=[pltpu.VMEM(term.shape, term.dtype)] * 3 + [sem] * 7,
+        compiler_params=pltpu.CompilerParams(collective_id=0, has_side_effects=True),
+        name="tensor_sum",
+    )(term)
+
+
+def owner_sum_kernel(n, rows, x_ref, out_ref, held, send_sem, recv_sem):
+    me = lax.axis_index("ctx")
+    barrier = pltpu.get_barrier_semaphore()
+    for step in range(1, n):
+        pl.semaphore_signal(
+            barrier, inc=1, device_id={"ctx": lax.rem(me + step, n)}, device_id_type=MESH
+        )
+    pl.semaphore_wait(barrier, n - 1)
+    copies = []
+    for step in range(1, n):
+        peer = lax.rem(me + step, n)
+        copy = pltpu.make_async_remote_copy(
+            src_ref=x_ref.at[pl.ds(pl.multiple_of(peer * rows, rows), rows)],
+            dst_ref=held.at[step - 1],
+            send_sem=send_sem.at[step - 1],
+            recv_sem=recv_sem.at[step - 1],
+            device_id={"ctx": peer},
+            device_id_type=MESH,
+        )
+        copy.start()
+        copies.append(copy)
+    own = pl.ds(pl.multiple_of(me * rows, rows), rows)
+    out_ref[...] = x_ref[own].astype(jnp.float32)
+    for step in range(1, n):
+        copies[step - 1].wait_recv()
+        out_ref[...] += held[step - 1].astype(jnp.float32)
+    for copy in copies:
+        copy.wait_send()
+
+
+def owner_sum(parts):
+    n = lax.axis_size("ctx")
+    if n == 1:
+        return parts.astype(jnp.float32)
+    total_rows, columns = parts.shape
+    rows = total_rows // n
+    sem = pltpu.SemaphoreType.DMA((n - 1,))
+    return pl.pallas_call(
+        functools.partial(owner_sum_kernel, n, rows),
+        out_shape=jax.ShapeDtypeStruct((rows, columns), jnp.float32),
+        in_specs=[pl.BlockSpec(memory_space=pltpu.VMEM)],
+        out_specs=pl.BlockSpec(memory_space=pltpu.VMEM),
+        scratch_shapes=[pltpu.VMEM((n - 1, rows, columns), parts.dtype), sem, sem],
+        compiler_params=pltpu.CompilerParams(collective_id=1, has_side_effects=True),
+        name="owner_sum",
+    )(parts)
 
 
 def passed_along(shard, axis, by):
@@ -113,14 +314,10 @@
         * softmax_scale
     ).reshape(queries.shape)
     key_part, value_part = key_side(query_heads, grad_heads, prob_full, score_grad, keys_all.shape)
-    key_grad, value_grad = (
-        lax.psum_scatter(
-            key_part.astype(jnp.bfloat16), "ctx", scatter_dimension=1, tiled=True
-        ).astype(jnp.float32),
-        lax.psum_scatter(
-            value_part.astype(jnp.bfloat16), "ctx", scatter_dimension=1, tiled=True
-        ).astype(jnp.float32),
-    )
+    cols = queries.shape[-1]
+    both = jnp.concatenate([key_part, value_part], axis=-1).astype(jnp.bfloat16)
+    owned = owner_sum(both.reshape(-1, 2 * cols)).reshape(*queries.shape[:2], 2 * cols)
+    key_grad, value_grad = owned[..., :cols], owned[..., cols:]
     return (query_grad, key_grad, value_grad)
 
 
@@ -142,16 +339,16 @@
     queries = (projected[:, :, 0] + b_qv[0]).astype(jnp.bfloat16)
     key_rows = projected[:, :, 1].astype(jnp.bfloat16)
     values = (projected[:, :, 2] + b_qv[1]).astype(jnp.bfloat16)
-    keys_all, values_all = (
-        lax.all_gather(key_rows, "ctx", axis=1, tiled=True),
-        lax.all_gather(values, "ctx", axis=1, tiled=True),
-    )
+    both = lax.all_gather(
+        jnp.concatenate([key_rows, values], axis=-1), "ctx", axis=1, tiled=True
+    )
+    keys_all, values_all = both[..., :local_cols], both[..., local_cols:]
     context, log_total = attend(queries, keys_all, values_all)
     attn_term = jnp.dot(
         context.reshape(row_count, local_cols), w_out, preferred_element_type=jnp.float32
     )
     attn_out = (
-        lax.psum(attn_term.astype(jnp.bfloat16), "tensor")
+        tensor_sum(attn_term.astype(jnp.bfloat16))
         .astype(jnp.float32)
         .reshape(block_in.shape)
         + b_out
@@ -168,7 +365,7 @@
     hidden = jax.nn.gelu(pre_act, approximate=True).astype(jnp.bfloat16)
     mlp_term = jnp.dot(hidden, w_fc2, preferred_element_type=jnp.float32)
     mlp_out = (
-        lax.psum(mlp_term.astype(jnp.bfloat16), "tensor")
+        tensor_sum(mlp_term.astype(jnp.bfloat16))
         .astype(jnp.float32)
         .reshape(block_in.shape)
         + b_fc2
@@ -219,18 +416,13 @@
     gate_m_grad = jnp.sum(upstream * mlp_out, axis=1)
     mlp_grad = upstream * mod_rows[:, 5, None, :]
     mlp_grad_b = mlp_grad.reshape(row_count, model_width).astype(jnp.bfloat16)
-    grad_w2 = jnp.dot(hidden.T, mlp_grad_b, preferred_element_type=jnp.float32)
     grad_b2 = jnp.sum(mlp_grad, axis=(0, 1))
     pre_grad = gelu_back(pre_act, jnp.dot(mlp_grad_b, w_fc2.T, preferred_element_type=jnp.float32))
     pre_grad_b = pre_grad.astype(jnp.bfloat16)
-    grad_w1 = jnp.dot(
-        mlp_in.reshape(row_count, model_width).T, pre_grad_b, preferred_element_type=jnp.float32
-    )
     grad_b1 = jnp.sum(pre_grad, axis=0)
     mlp_in_grad = (
-        lax.psum(
-            jnp.dot(pre_grad_b, w_fc1.T, preferred_element_type=jnp.float32).astype(jnp.bfloat16),
-            "tensor",
+        tensor_sum(
+            jnp.dot(pre_grad_b, w_fc1.T, preferred_element_type=jnp.float32).astype(jnp.bfloat16)
         )
         .astype(jnp.float32)
         .reshape(upstream.shape)
@@ -243,9 +435,6 @@
     gate_a_grad = jnp.sum(middle_grad * attn_out, axis=1)
     attn_grad = middle_grad * mod_rows[:, 2, None, :]
     attn_grad_b = attn_grad.reshape(row_count, model_width).astype(jnp.bfloat16)
-    grad_wo = jnp.dot(
-        context.reshape(row_count, local_cols).T, attn_grad_b, preferred_element_type=jnp.float32
-    )
     grad_bo = jnp.sum(attn_grad, axis=(0, 1))
     context_grad = (
         jnp.dot(attn_grad_b, w_out.T, preferred_element_type=jnp.float32)
@@ -261,17 +450,13 @@
         .astype(jnp.bfloat16)
         .reshape(row_count, 3 * local_cols)
     )
-    grad_wqkv = jnp.dot(
-        attn_in.reshape(row_count, model_width).T, qkv_grad_b, preferred_element_type=jnp.float32
-    ).reshape(model_width, 3, local_cols)
     attn_in_grad = (
-        lax.psum(
+        tensor_sum(
             jnp.dot(
                 qkv_grad_b,
                 w_qkv.reshape(model_width, 3 * local_cols).T,
                 preferred_element_type=jnp.float32,
-            ).astype(jnp.bfloat16),
-            "tensor",
+            ).astype(jnp.bfloat16)
         )
         .astype(jnp.float32)
         .reshape(upstream.shape)
@@ -287,7 +472,13 @@
     return (
         input_grad,
         mod_grad,
-        (grad_wqkv, grad_bqv, grad_wo, grad_bo, grad_w1, grad_b1, grad_w2, grad_b2),
+        (grad_bqv, grad_bo, grad_b1, grad_b2),
+        (
+            (attn_in.reshape(row_count, model_width), qkv_grad_b),
+            (context.reshape(row_count, local_cols), attn_grad_b),
+            (mlp_in.reshape(row_count, model_width), pre_grad_b),
+            (hidden, mlp_grad_b),
+        ),
     )
 
 
@@ -337,19 +528,13 @@
             received = passed_along(block_res, "section", 1)
     in_grads = jnp.zeros(latents.shape, jnp.float32)
     mod_grads = jnp.zeros((latent_total, width_cols), jnp.float32)
-    big_local = tuple(
-        (
-            jnp.zeros(weight.shape, jnp.float32)
-            for weight in (weights[0], weights[2], weights[4], weights[6])
-        )
-    )
+    pairs = []
     small_local = tuple(
         (
             jnp.zeros(weight.shape, jnp.float32)
             for weight in (weights[1], weights[3], weights[5], weights[7])
         )
     )
-    shares = None
     grad_received = jnp.zeros((MB, token_count, model_width), jnp.float32)
     for back_tick in range(NMB + 1):
         forward_tick = NMB - back_tick
@@ -360,7 +545,15 @@
         upstream = jnp.where(section_index == 1, own_cot, grad_received)
         mod_rows = lax.dynamic_slice_in_dim(modulation, offset, MB, 0)
         stored = kept_states[forward_tick]
-        input_grad, mod_grad, grad_terms = backward_block(upstream, stored, mod_rows, weights)
+        input_grad, mod_grad, grad_terms, grad_pairs = backward_block(
+            upstream, stored, mod_rows, weights
+        )
+        pairs.append(
+            tuple(
+                (left, jnp.where(is_valid, right, jnp.zeros_like(right)))
+                for left, right in grad_pairs
+            )
+        )
         masked = tuple((jnp.where(is_valid, term, 0.0) for term in grad_terms))
         previous = lax.dynamic_slice_in_dim(in_grads, offset, MB, 0)
         in_grads = lax.dynamic_update_slice_in_dim(
@@ -373,22 +566,20 @@
         mod_grads = lax.dynamic_update_slice_in_dim(
             mod_grads, jnp.where(is_valid, mod_piece, prior), offset, 0
         )
-        small_local = (
-            small_local[0] + masked[1],
-            small_local[1] + masked[3],
-            small_local[2] + masked[5],
-            small_local[3] + masked[7],
-        )
-        big_local = (
-            big_local[0] + masked[0],
-            big_local[1] + masked[2],
-            big_local[2] + masked[4],
-            big_local[3] + masked[6],
-        )
+        small_local = tuple(total + term for total, term in zip(small_local, masked))
         if back_tick < NMB:
             grad_received = passed_along(input_grad.astype(jnp.bfloat16), "section", -1).astype(
                 input_grad.dtype
             )
+    big_local = tuple(
+        jnp.dot(
+            jnp.concatenate([tick[which][0] for tick in pairs], axis=0).T,
+            jnp.concatenate([tick[which][1] for tick in pairs], axis=0),
+            preferred_element_type=jnp.float32,
+        )
+        for which in range(4)
+    )
+    big_local = (big_local[0].reshape(weights[0].shape),) + big_local[1:]
     shares = (
         lax.psum_scatter(
             big_local[0].astype(jnp.bfloat16), "ctx", scatter_dimension=0, tiled=True

time: 1320 us -> 1080 us (0.82)
  waiting for transfers between devices: 817 us -> 114 us
  Pallas kernels: 0 us -> 496 us
  blocking collectives: 120 us -> 59.8 us
  matrix products: 168 us -> 119 us
  other arithmetic: 104 us -> 143 us
  local copies, waits for them, and re-layouts: 66.8 us -> 104 us
    psum x15 -> x0, waiting for transfers between devices: 547 us -> none  [the longest x4 155 us: forward_block(): lax.psum(attn_term.astype(jnp.bfloat16), 'tensor').astype(jnp.float32)]
    pallas_call x0 -> x20, Pallas kernels: none -> 496 us  [the longest x16 421 us: tensor_sum(): pl.pallas_call(functools.partial(line_sum_kernel, n, PIECES, rows), out_s...]
    reduce_scatter x8 -> x1, waiting for transfers between devices: 140 us -> 0.01 us  [local(): lax.psum_scatter(big_local[3].astype(jnp.bfloat16), 'ctx', scatter_dimens...]
    all_gather x0 -> x4, waiting for transfers between devices: none -> 61.2 us  [forward_block(): lax.all_gather(jnp.concatenate([key_rows, values], axis=-1), 'ctx', axis=...]
    all_gather x8 -> x0, blocking collectives: 59.9 us -> none  [the longest x4 30.6 us: forward_block(): lax.all_gather(values, 'ctx', axis=1, tiled=True)]
    reduce_scatter x1, waiting for transfers between devices: 34.8 us -> 0.01 us  [local(): lax.psum_scatter(big_local[0].astype(jnp.bfloat16), 'ctx', scatter_dimens...]
    dot_general x16 -> x4, matrix products: 47.8 us -> 18.8 us  [local(): jnp.dot(jnp.concatenate([tick[which][0] for tick in pairs], axis=0).T, jn...]
    ppermute x6, waiting for transfers between devices: 80.6 us -> 52.7 us  [passed_along(): return lax.ppermute(shard, axis, pairs)]
  transfers between devices with their start and end apart: 33 -> 14, of which waited for: 30 -> 9; matrix products, arithmetic and copies ran while one was open for 11% -> 11% of each run, Pallas kernels for 0% -> 7%
where the time goes in v1:
time: 1080 us; the launch traced here: 1070 us
  Pallas kernels  496 us (46%)
  other arithmetic  143 us (13%)
  matrix products  119 us (11%)
  waiting for transfers between devices  114 us (11%)
  local copies, waits for them, and re-layouts  104 us (10%)
  blocking collectives  59.8 us (6%)
  between operations  18.2 us (2%)
  starting transfers between devices  16.7 us (2%)
    pallas_call x16, Pallas kernels, tensor_sum(): pl.pallas_call(functools.partial(line_sum_kernel, n, PIECES, rows), out_s...  421 us
    pallas_call x4, Pallas kernels, owner_sum(): pl.pallas_call(functools.partial(owner_sum_kernel, n, rows), out_shape=ja...  75.2 us
    all_gather x4, waiting for transfers between devices, forward_block(): lax.all_gather(jnp.concatenate([key_rows, values], axis=-1), 'ctx', axis=...  61.2 us
    ppermute x6, waiting for transfers between devices, passed_along(): return lax.ppermute(shard, axis, pairs)  52.7 us
    unnamed x571, local copies, waits for them, and re-layouts  36.8 us
    select_n x10, other arithmetic, local(): jnp.where(is_valid, right, jnp.zeros_like(right))  24.1 us
    psum x1, blocking collectives, local(): cond_sum = lax.psum(cond_part, ('section', 'tensor'))  22 us
  transfers between devices with their start and end apart: 14, of which 9 were waited for; matrix products, arithmetic and copies ran while one was open for 11% of the time, Pallas kernels for 7%

profile of v1, /device:TPU:0, one launch (start us, length us, event | category | flops | bytes accessed | tf_op | source)
XLA Modules:
  0.0 1070.9 jit_solution(4524444411026614484)
XLA Ops:
  8.9 13.0 %psum.49 = f32[3,1728]{1,0:T(4,128)S(1)} all-reduce(f32[3,1728]{1,0:T(4,128)S(1)} %fusion.309), channel_id=1, replica_groups=mesh['section'=2,'tensor'=4,'ctx'=4] {'ctx'}, use_global_device_ids=true, to_apply=%region_0.1 | all-reduce | flops 5184 | bytes 41472 | tf_op jit(solution)/shard_map/psum | solution.py:507
  22.6 13.6 %all-gather = f32[4,1728,3]{1,2,0:T(4,128)S(1)} all-gather(f32[1,1728,3]{1,2,0:T(4,128)S(1)} %add_bitcast_fusion), channel_id=1, replica_groups=mesh['section'=2,'tensor'=4,'ctx'=4] {'tensor'}, dimensions={0}, use_global_device_ids=true | all-gather | bytes 103680 | tf_op jit(solution)/shard_map/all_gather | solution.py:508
  47.0 15.4 %all-gather.6.cloned.1.call-done = bf16[1,1024,576]{1,2,0:T(8,128)(2,1)} async-done(((bf16[1,256,576]{1,2,0:T(8,128)(2,1)}), bf16[1,1024,576]{1,2,0:T(8,128)(2,1)}) %all-gather.6.cloned.1.call-update) | async-done | bytes 1179664 | tf_op jit(solution)/shard_map/all_gather | solution.py:342
  69.6 27.8 %tensor_sum.16 = bf16[256,1152]{1,0:T(8,128)(2,1)} custom-call(bf16[256,1152]{1,0:T(8,128)(2,1)} %convolution_convert_fusion.7.x_ref), custom_call_target="tpu_custom_call" | custom-call | tf_op jit(solution)/shard_map/tensor_sum/pallas_call | solution.py:158
  106.8 25.8 %tensor_sum.17 = bf16[256,1152]{1,0:T(8,128)(2,1)} custom-call(bf16[256,1152]{1,0:T(8,128)(2,1)} %fusion.44.x_ref), custom_call_target="tpu_custom_call" | custom-call | tf_op jit(solution)/shard_map/tensor_sum/pallas_call | solution.py:158
  151.8 15.5 %all-gather.8.cloned.1.call-done = bf16[1,1024,576]{1,2,0:T(8,128)(2,1)} async-done(((bf16[1,256,576]{1,2,0:T(8,128)(2,1)}), bf16[1,1024,576]{1,2,0:T(8,128)(2,1)}) %all-gather.8.cloned.1.call-update) | async-done | bytes 1179664 | tf_op jit(solution)/shard_map/all_gather | solution.py:342
  174.6 27.8 %tensor_sum.18 = bf16[256,1152]{1,0:T(8,128)(2,1)} custom-call(bf16[256,1152]{1,0:T(8,128)(2,1)} %convolution_convert_fusion.6.x_ref), custom_call_target="tpu_custom_call" | custom-call | tf_op jit(solution)/shard_map/tensor_sum/pallas_call | solution.py:158
  209.7 25.8 %tensor_sum.19 = bf16[256,1152]{1,0:T(8,128)(2,1)} custom-call(bf16[256,1152]{1,0:T(8,128)(2,1)} %fusion.47.x_ref), custom_call_target="tpu_custom_call" | custom-call | tf_op jit(solution)/shard_map/tensor_sum/pallas_call | solution.py:158
  241.9 7.3 collective-permute-done.1
  255.5 15.3 %all-gather.10.cloned.1.call-done = bf16[1,1024,576]{1,2,0:T(8,128)(2,1)} async-done(((bf16[1,256,576]{1,2,0:T(8,128)(2,1)}), bf16[1,1024,576]{1,2,0:T(8,128)(2,1)}) %all-gather.10.cloned.1.call-update) | async-done | bytes 1179664 | tf_op jit(solution)/shard_map/all_gather | solution.py:342
  278.1 27.7 %tensor_sum.20 = bf16[256,1152]{1,0:T(8,128)(2,1)} custom-call(bf16[256,1152]{1,0:T(8,128)(2,1)} %convolution_convert_fusion.5.x_ref), custom_call_target="tpu_custom_call" | custom-call | tf_op jit(solution)/shard_map/tensor_sum/pallas_call | solution.py:158
  313.2 25.8 %tensor_sum.21 = bf16[256,1152]{1,0:T(8,128)(2,1)} custom-call(bf16[256,1152]{1,0:T(8,128)(2,1)} %fusion.50.x_ref), custom_call_target="tpu_custom_call" | custom-call | tf_op jit(solution)/shard_map/tensor_sum/pallas_call | solution.py:158
  345.3 7.3 collective-permute-done.2
  359.2 15.1 %all-gather.12.cloned.1.call-done = bf16[1,1024,576]{1,2,0:T(8,128)(2,1)} async-done(((bf16[1,256,576]{1,2,0:T(8,128)(2,1)}), bf16[1,1024,576]{1,2,0:T(8,128)(2,1)}) %all-gather.12.cloned.1.call-update) | async-done | bytes 1179664 | tf_op jit(solution)/shard_map/all_gather | solution.py:342
  381.5 27.8 %tensor_sum.22 = bf16[256,1152]{1,0:T(8,128)(2,1)} custom-call(bf16[256,1152]{1,0:T(8,128)(2,1)} %convolution_convert_fusion.4.x_ref), custom_call_target="tpu_custom_call" | custom-call | tf_op jit(solution)/shard_map/tensor_sum/pallas_call | solution.py:158
  419.5 26.0 %tensor_sum.24 = bf16[256,1152]{1,0:T(8,128)(2,1)} custom-call(bf16[256,1152]{1,0:T(8,128)(2,1)} %fusion.32.x_ref), custom_call_target="tpu_custom_call" | custom-call | tf_op jit(solution)/shard_map/tensor_sum/pallas_call | solution.py:158
  469.1 17.3 %owner_sum.4 = f32[256,576]{1,0:T(8,128)} custom-call(bf16[1024,576]{1,0:T(8,128)(2,1)} %pad_maximum_fusion.x_ref), custom_call_target="tpu_custom_call" | custom-call | tf_op jit(solution)/shard_map/owner_sum/pallas_call | solution.py:206
  491.7 25.9 %tensor_sum.25 = bf16[256,1152]{1,0:T(8,128)(2,1)} custom-call(bf16[256,1152]{1,0:T(8,128)(2,1)} %fusion.56.x_ref), custom_call_target="tpu_custom_call" | custom-call | tf_op jit(solution)/shard_map/tensor_sum/pallas_call | solution.py:158
  526.1 15.0 %collective-permute-done.3 = bf16[1,256,1152]{2,1,0:T(8,128)(2,1)S(1)} collective-permute-done((bf16[1,256,1152]{2,1,0:T(8,128)(2,1)S(1)}, bf16[1,256,1152]{2,1,0:T(8,128)(2,1)S(1)}, u32[]{:S(2)}, u32[]{:S(2)}) %collective-permute-start.3) | collective-permute-done | bytes 589856 | tf_op jit(solution)/shard_map/ppermute | solution.py:220
  547.0 25.3 %tensor_sum.26 = bf16[256,1152]{1,0:T(8,128)(2,1)} custom-call(bf16[256,1152]{1,0:T(8,128)(2,1)} %fusion.35.x_ref), custom_call_target="tpu_custom_call" | custom-call | tf_op jit(solution)/shard_map/tensor_sum/pallas_call | solution.py:158
  597.7 17.1 %owner_sum.5 = f32[256,576]{1,0:T(8,128)} custom-call(bf16[1024,576]{1,0:T(8,128)(2,1)} %pad_maximum_fusion.1.x_ref), custom_call_target="tpu_custom_call" | custom-call | tf_op jit(solution)/shard_map/owner_sum/pallas_call | solution.py:206
  620.1 26.0 %tensor_sum.27 = bf16[256,1152]{1,0:T(8,128)(2,1)} custom-call(bf16[256,1152]{1,0:T(8,128)(2,1)} %fusion.57.x_ref), custom_call_target="tpu_custom_call" | custom-call | tf_op jit(solution)/shard_map/tensor_sum/pallas_call | solution.py:158
  654.5 15.8 %collective-permute-done.4 = bf16[1,256,1152]{2,1,0:T(8,128)(2,1)S(1)} collective-permute-done((bf16[1,256,1152]{2,1,0:T(8,128)(2,1)S(1)}, bf16[1,256,1152]{2,1,0:T(8,128)(2,1)S(1)}, u32[]{:S(2)}, u32[]{:S(2)}) %collective-permute-start.4) | collective-permute-done | bytes 589856 | tf_op jit(solution)/shard_map/ppermute | solution.py:220
  676.3 25.5 %tensor_sum.28 = bf16[256,1152]{1,0:T(8,128)(2,1)} custom-call(bf16[256,1152]{1,0:T(8,128)(2,1)} %fusion.38.x_ref), custom_call_target="tpu_custom_call" | custom-call | tf_op jit(solution)/shard_map/tensor_sum/pallas_call | solution.py:158
  727.8 17.2 %owner_sum.6 = f32[256,576]{1,0:T(8,128)} custom-call(bf16[1024,576]{1,0:T(8,128)(2,1)} %pad_maximum_fusion.2.x_ref), custom_call_target="tpu_custom_call" | custom-call | tf_op jit(solution)/shard_map/owner_sum/pallas_call | solution.py:206
  750.2 25.8 %tensor_sum.29 = bf16[256,1152]{1,0:T(8,128)(2,1)} custom-call(bf16[256,1152]{1,0:T(8,128)(2,1)} %fusion.58.x_ref), custom_call_target="tpu_custom_call" | custom-call | tf_op jit(solution)/shard_map/tensor_sum/pallas_call | solution.py:158
  809.5 26.3 %tensor_sum.30 = bf16[256,1152]{1,0:T(8,128)(2,1)} custom-call(bf16[256,1152]{1,0:T(8,128)(2,1)} %fusion.41.x_ref), custom_call_target="tpu_custom_call" | custom-call | tf_op jit(solution)/shard_map/tensor_sum/pallas_call | solution.py:158
  864.6 23.5 %owner_sum.7 = f32[256,576]{1,0:T(8,128)} custom-call(bf16[1024,576]{1,0:T(8,128)(2,1)} %pad_maximum_fusion.3.x_ref), custom_call_target="tpu_custom_call" | custom-call | tf_op jit(solution)/shard_map/owner_sum/pallas_call | solution.py:206
  899.5 26.3 %tensor_sum.31 = bf16[256,1152]{1,0:T(8,128)(2,1)} custom-call(bf16[256,1152]{1,0:T(8,128)(2,1)} %fusion.59.x_ref), custom_call_target="tpu_custom_call" | custom-call | tf_op jit(solution)/shard_map/tensor_sum/pallas_call | solution.py:158
  949.5 25.7 %tensor_sum.23 = bf16[256,1152]{1,0:T(8,128)(2,1)} custom-call(bf16[256,1152]{1,0:T(8,128)(2,1)} %fusion.53.x_ref), custom_call_target="tpu_custom_call" | custom-call | tf_op jit(solution)/shard_map/tensor_sum/pallas_call | solution.py:158
  1014.5 11.1 %all-reduce = (f32[3,1728]{1,0:T(4,128)S(1)}, f32[1,2,288]{2,1,0:T(2,128)}, f32[1,1152]{1,0:T(1,128)}, f32[1,1152]{1,0:T(1,128)}, f32[1,1152]{1,0:T(1,128)}) all-reduce(f32[3,1728]{1,0:T(4,128)S(1)} %dynamic_update_slice.49, f32[1,2,288]{2,1,0:T(2,128)S(1)} %fusion.456, ...), channel_id=1, replica_groups=mesh['section'=2,'tensor'=4,'ctx'=4] {'ctx'}, use_global_device_ids=true, to_apply=%region_69.70 | all-reduce | flops 9216 | bytes 73728 | tf_op jit(solution)/shard_map/psum | solution.py:597
  1027.8 22.0 %psum.51 = f32[3,288]{1,0:T(4,128)S(1)} all-reduce(f32[3,288]{1,0:T(4,128)S(1)} %fusion.307), channel_id=1, replica_groups=mesh['section'=2,'tensor'=4,'ctx'=4] {'section','tensor'}, use_global_device_ids=true, to_apply=%region_70.71 | all-reduce | flops 864 | bytes 6912 | tf_op jit(solution)/shard_map/psum | solution.py:605
  (887 shorter events, 389.7 us)
Async XLA Ops:
  7.2 94.9 %copy-start = (bf16[1,1152,1152]{2,1,0:T(8,128)(2,1)S(1)}, bf16[1,1152,1152]{2,1,0:T(8,128)(2,1)}, u32[]{:S(2)}) copy-start(bf16[1,1152,1152]{2,1,0:T(8,128)(2,1)} %param.22) | copy-start | bytes 7962628
  7.2 55.2 %all-gather.6.cloned.1.call-start = ((), (), s32[]{:S(2)}) async-start(), calls=%async_computation.4 | async-start | bytes 1474560 | tf_op jit(solution)/shard_map/all_gather | solution.py:342
  8.9 30.3 %copy-start.264 = (f32[1,2,288]{2,1,0:T(2,128)S(1)}, f32[1,2,288]{2,1,0:T(2,128)}, u32[]{:S(2)}) copy-start(f32[1,2,288]{2,1,0:T(2,128)} %param.19) | copy-start | bytes 6916
  44.6 122.7 %all-gather.8.cloned.1.call-start = ((), (), s32[]{:S(2)}) async-start(), calls=%async_computation.5 | async-start | bytes 1474560 | tf_op jit(solution)/shard_map/all_gather | solution.py:342
  135.8 11.0 %collective-permute-start = (bf16[1,256,1152]{2,1,0:T(8,128)(2,1)S(1)}, bf16[1,256,1152]{2,1,0:T(8,128)(2,1)S(1)}, u32[]{:S(2)}, u32[]{:S(2)}) collective-permute-start(bf16[1,256,1152]{2,1,0:T(8,128)(2,1)S(1)} %get-tuple-element.127), channel_id=1, source_target_pairs={{0,16},{1,17},{2,18},{3,19},{4,20},{5,21},{6,22},{7,23},{8,24},{9,... | collective-permute-start | bytes 1769480 | tf_op jit(solution)/shard_map/ppermute | solution.py:220
  147.1 88.5 %copy-start.9 = (bf16[1,256,1152]{2,1,0:T(8,128)(2,1)}, bf16[1,256,1152]{2,1,0:T(8,128)(2,1)S(1)}, u32[]{:S(2)}) copy-start(bf16[1,256,1152]{2,1,0:T(8,128)(2,1)S(1)} %get-tuple-element.125) | copy-start | bytes 1769476
  150.1 120.7 %all-gather.10.cloned.1.call-start = ((), (), s32[]{:S(2)}) async-start(), calls=%async_computation.6 | async-start | bytes 1474560 | tf_op jit(solution)/shard_map/all_gather | solution.py:342
  238.3 10.9 %collective-permute-start.1 = (bf16[1,256,1152]{2,1,0:T(8,128)(2,1)S(1)}, bf16[1,256,1152]{2,1,0:T(8,128)(2,1)S(1)}, u32[]{:S(2)}, u32[]{:S(2)}) collective-permute-start(bf16[1,256,1152]{2,1,0:T(8,128)(2,1)S(1)} %get-tuple-element.123), channel_id=1, source_target_pairs={{0,16},{1,17},{2,18},{3,19},{4,20},{5,21},{6,22},{7,23},{8,24},{9,... | collective-permute-start | bytes 1769480 | tf_op jit(solution)/shard_map/ppermute | solution.py:220
  250.5 88.5 %copy-start.12 = (bf16[1,256,1152]{2,1,0:T(8,128)(2,1)}, bf16[1,256,1152]{2,1,0:T(8,128)(2,1)S(1)}, u32[]{:S(2)}) copy-start(bf16[1,256,1152]{2,1,0:T(8,128)(2,1)S(1)} %get-tuple-element.121) | copy-start | bytes 1769476
  253.6 120.7 %all-gather.12.cloned.1.call-start = ((), (), s32[]{:S(2)}) async-start(), calls=%async_computation.7 | async-start | bytes 1474560 | tf_op jit(solution)/shard_map/all_gather | solution.py:342
  341.8 10.9 %collective-permute-start.2 = (bf16[1,256,1152]{2,1,0:T(8,128)(2,1)S(1)}, bf16[1,256,1152]{2,1,0:T(8,128)(2,1)S(1)}, u32[]{:S(2)}, u32[]{:S(2)}) collective-permute-start(bf16[1,256,1152]{2,1,0:T(8,128)(2,1)S(1)} %get-tuple-element.119), channel_id=1, source_target_pairs={{0,16},{1,17},{2,18},{3,19},{4,20},{5,21},{6,22},{7,23},{8,24},{9,... | collective-permute-start | bytes 1769480 | tf_op jit(solution)/shard_map/ppermute | solution.py:220
  357.0 698.2 %reduce-scatter.13.cloned.1.call-start = ((), (), s32[]{:S(2)}) async-start(), calls=%async_computation.11 | async-start | bytes 1105920
  524.4 16.7 %collective-permute-start.3 = (bf16[1,256,1152]{2,1,0:T(8,128)(2,1)S(1)}, bf16[1,256,1152]{2,1,0:T(8,128)(2,1)S(1)}, u32[]{:S(2)}, u32[]{:S(2)}) collective-permute-start(bf16[1,256,1152]{2,1,0:T(8,128)(2,1)S(1)} %get-tuple-element.114), channel_id=1, source_target_pairs={{16,0},{17,1},{18,2},{19,3},{20,4},{21,5},{22,6},{23,7},{24,8},{25... | collective-permute-start | bytes 1769480 | tf_op jit(solution)/shard_map/ppermute | solution.py:220
  651.6 18.7 %copy-start.168 = (f32[1152]{0:T(1024)S(1)}, f32[1152]{0:T(1024)}, u32[]{:S(2)}) copy-start(f32[1152]{0:T(1024)} %get-tuple-element.76) | copy-start | bytes 13828
  653.2 17.1 %collective-permute-start.4 = (bf16[1,256,1152]{2,1,0:T(8,128)(2,1)S(1)}, bf16[1,256,1152]{2,1,0:T(8,128)(2,1)S(1)}, u32[]{:S(2)}, u32[]{:S(2)}) collective-permute-start(bf16[1,256,1152]{2,1,0:T(8,128)(2,1)S(1)} %get-tuple-element.112), channel_id=1, source_target_pairs={{16,0},{17,1},{18,2},{19,3},{20,4},{21,5},{22,6},{23,7},{24,8},{25... | collective-permute-start | bytes 1769480 | tf_op jit(solution)/shard_map/ppermute | solution.py:220
  783.2 19.3 %collective-permute-start.5 = (bf16[1,256,1152]{2,1,0:T(8,128)(2,1)}, bf16[1,256,1152]{2,1,0:T(8,128)(2,1)}, u32[]{:S(2)}, u32[]{:S(2)}) collective-permute-start(bf16[1,256,1152]{2,1,0:T(8,128)(2,1)} %get-tuple-element.110), channel_id=1, source_target_pairs={{16,0},{17,1},{18,2},{19,3},{20,4},{21,5},{22,6},{23,7},{24,8},{25... | collective-permute-start | bytes 1769480 | tf_op jit(solution)/shard_map/ppermute | solution.py:220
  857.1 200.1 %reduce-scatter.7.cloned.1.call-start = ((), (), s32[]{:S(2)}) async-start(), calls=%async_computation.8 | async-start | bytes 3317760 | tf_op jit(solution)/shard_map/reduce_scatter | solution.py:584
  864.6 25.6 %copy-start.100 = (bf16[1,256,4,72]{1,3,2,0:T(8,128)(2,1)S(1)}, bf16[1,256,4,72]{1,3,2,0:T(8,128)(2,1)}, u32[]{:S(2)}) copy-start(bf16[1,256,4,72]{1,3,2,0:T(8,128)(2,1)} %get-tuple-element.167) | copy-start | bytes 442372
  899.5 26.3 %copy-start.136 = (f32[1152]{0:T(1024)S(1)}, f32[1152]{0:T(1024)}, u32[]{:S(2)}) copy-start(f32[1152]{0:T(1024)} %copy-done.135) | copy-start | bytes 13828
  899.5 26.3 %copy-start.187 = (f32[1152]{0:T(1024)S(1)}, f32[1152]{0:T(1024)}, u32[]{:S(2)}) copy-start(f32[1152]{0:T(1024)} %copy-done.186) | copy-start | bytes 13828
  899.5 26.3 %copy-start.224 = (f32[256]{0:T(256)S(1)}, f32[256]{0:T(256)}, u32[]{:S(2)}) copy-start(f32[256]{0:T(256)} %copy-done.223) | copy-start | bytes 3076
  899.5 26.3 %copy-start.240 = (f32[256]{0:T(256)S(1)}, f32[256]{0:T(256)}, u32[]{:S(2)}) copy-start(f32[256]{0:T(256)} %copy-done.239) | copy-start | bytes 3076
  937.3 122.1 %reduce-scatter.11.cloned.1.call-start = ((), (), s32[]{:S(2)}) async-start(), calls=%async_computation.10 | async-start | bytes 3317760 | tf_op jit(solution)/shard_map/reduce_scatter | solution.py:593
  944.5 117.2 %reduce-scatter.9.cloned.1.call-start = ((), (), s32[]{:S(2)}) async-start(), calls=%async_computation.9 | async-start | bytes 3317760 | tf_op jit(solution)/shard_map/reduce_scatter | solution.py:590
  949.5 25.7 %copy-start.247 = (f32[4,72]{1,0:T(4,128)S(1)}, f32[4,72]{1,0:T(4,128)}, u32[]{:S(2)}) copy-start(f32[4,72]{1,0:T(4,128)} %get-tuple-element.160) | copy-start | bytes 3460
  949.5 27.0 %copy-start.197 = (f32[1152]{0:T(1024)S(1)}, f32[1152]{0:T(1024)}, u32[]{:S(2)}) copy-start(f32[1152]{0:T(1024)} %get-tuple-element.63) | copy-start | bytes 13828
  949.5 27.0 %copy-start.199 = (f32[1152]{0:T(1024)S(1)}, f32[1152]{0:T(1024)}, u32[]{:S(2)}) copy-start(f32[1152]{0:T(1024)} %get-tuple-element.39) | copy-start | bytes 13828
  949.5 27.0 %copy-start.195 = (f32[1152]{0:T(1024)S(1)}, f32[1152]{0:T(1024)}, u32[]{:S(2)}) copy-start(f32[1152]{0:T(1024)} %get-tuple-element.27) | copy-start | bytes 13828
  949.5 27.1 %copy-start.196 = (f32[1152]{0:T(1024)S(1)}, f32[1152]{0:T(1024)}, u32[]{:S(2)}) copy-start(f32[1152]{0:T(1024)} %get-tuple-element.61) | copy-start | bytes 13828
  1011.4 38.4 %copy-start.181 = (f32[3,288]{1,0:T(4,128)S(1)}, f32[3,288]{1,0:T(4,128)}, u32[]{:S(2)}) copy-start(f32[3,288]{1,0:T(4,128)} %param.14) | copy-start | bytes 10372
  1027.8 23.9 %copy-start.263 = (f32[256]{0:T(256)S(1)}, f32[256]{0:T(256)}, u32[]{:S(2)}) copy-start(f32[256]{0:T(256)} %get-tuple-element.52) | copy-start | bytes 3076
  1027.8 23.9 %copy-start.262 = (f32[256]{0:T(256)S(1)}, f32[256]{0:T(256)}, u32[]{:S(2)}) copy-start(f32[256]{0:T(256)} %get-tuple-element.16) | copy-start | bytes 3076
  (263 other events, 882.0 us)
Sparse Core Ops, SparseCore 0:
  44.7 17.6 all-gather.5
  150.2 17.0 all-gather.7
  253.7 17.0 all-gather.9
  357.1 17.0 all-gather.11
  857.2 29.9 reduce-scatter.12
  937.4 34.1 reduce-scatter.6
  974.2 34.7 reduce-scatter.10
  1011.5 34.7 reduce-scatter.8

commit v2 on v1

--- a/solution.py
+++ b/solution.py
@@ -17,7 +17,8 @@
 
 
 MESH = pl.DeviceIdType.MESH
-PIECES = 2
+PIECES = 4
+PIECE_ROWS = 16
 
 
 def line_role(d, n, pieces, rows, x_ref, out_ref, acc, buf_l, buf_r, sems):
@@ -153,10 +154,11 @@
     if n == 1:
         return term
     total_rows, columns = term.shape
-    rows = total_rows // (n * PIECES)
-    sem = pltpu.SemaphoreType.DMA((n, PIECES))
+    pieces = max(1, min(PIECES, total_rows // (n * PIECE_ROWS)))
+    rows = total_rows // (n * pieces)
+    sem = pltpu.SemaphoreType.DMA((n, pieces))
     return pl.pallas_call(
-        functools.partial(line_sum_kernel, n, PIECES, rows),
+        functools.partial(line_sum_kernel, n, pieces, rows),
         out_shape=jax.ShapeDtypeStruct(term.shape, term.dtype),
         in_specs=[pl.BlockSpec(memory_space=pltpu.VMEM)],
         out_specs=pl.BlockSpec(memory_space=pltpu.VMEM),

time: 1080 us -> 1130 us (1.046)
  Pallas kernels: 496 us -> 551 us
    pallas_call x16, Pallas kernels: 421 us -> 476 us  [tensor_sum(): pl.pallas_call(functools.partial(line_sum_kernel, n, pieces, rows), out_s...]
  transfers between devices with their start and end apart: 14 -> 14, of which waited for: 9 -> 9; matrix products, arithmetic and copies ran while one was open for 11% -> 10% of each run, Pallas kernels for 7% -> 7%
where the time goes in v2:
time: 1130 us; the launch traced here: 1120 us
  Pallas kernels  551 us (49%)
  other arithmetic  142 us (13%)
  matrix products  119 us (11%)
  waiting for transfers between devices  110 us (10%)
  local copies, waits for them, and re-layouts  104 us (9%)
  blocking collectives  61 us (5%)
  between operations  18.2 us (2%)
  starting transfers between devices  16.5 us (1%)
    pallas_call x16, Pallas kernels, tensor_sum(): pl.pallas_call(functools.partial(line_sum_kernel, n, pieces, rows), out_s...  476 us
    pallas_call x4, Pallas kernels, owner_sum(): pl.pallas_call(functools.partial(owner_sum_kernel, n, rows), out_shape=ja...  74.8 us
    all_gather x4, waiting for transfers between devices, forward_block(): lax.all_gather(jnp.concatenate([key_rows, values], axis=-1), 'ctx', axis=...  60.9 us
    ppermute x6, waiting for transfers between devices, passed_along(): return lax.ppermute(shard, axis, pairs)  48.5 us
    unnamed x571, local copies, waits for them, and re-layouts  37.2 us
    select_n x10, other arithmetic, local(): jnp.where(is_valid, right, jnp.zeros_like(right))  23.8 us
    psum x1, blocking collectives, local(): cond_sum = lax.psum(cond_part, ('section', 'tensor'))  23.2 us
  transfers between devices with their start and end apart: 14, of which 9 were waited for; matrix products, arithmetic and copies ran while one was open for 10% of the time, Pallas kernels for 7%

profile of v2, /device:TPU:0, one launch (start us, length us, event | category | flops | bytes accessed | tf_op | source)
XLA Modules:
  0.0 1121.9 jit_solution(3342783072320810112)
XLA Ops:
  8.9 13.0 %psum.49 = f32[3,1728]{1,0:T(4,128)S(1)} all-reduce(f32[3,1728]{1,0:T(4,128)S(1)} %fusion.309), channel_id=1, replica_groups=mesh['section'=2,'tensor'=4,'ctx'=4] {'ctx'}, use_global_device_ids=true, to_apply=%region_0.1 | all-reduce | flops 5184 | bytes 41472 | tf_op jit(solution)/shard_map/psum | solution.py:509
  22.6 13.6 %all-gather = f32[4,1728,3]{1,2,0:T(4,128)S(1)} all-gather(f32[1,1728,3]{1,2,0:T(4,128)S(1)} %add_bitcast_fusion), channel_id=1, replica_groups=mesh['section'=2,'tensor'=4,'ctx'=4] {'tensor'}, dimensions={0}, use_global_device_ids=true | all-gather | bytes 103680 | tf_op jit(solution)/shard_map/all_gather | solution.py:510
  47.0 15.4 %all-gather.6.cloned.1.call-done = bf16[1,1024,576]{1,2,0:T(8,128)(2,1)} async-done(((bf16[1,256,576]{1,2,0:T(8,128)(2,1)}), bf16[1,1024,576]{1,2,0:T(8,128)(2,1)}) %all-gather.6.cloned.1.call-update) | async-done | bytes 1179664 | tf_op jit(solution)/shard_map/all_gather | solution.py:344
  69.6 31.5 %tensor_sum.16 = bf16[256,1152]{1,0:T(8,128)(2,1)} custom-call(bf16[256,1152]{1,0:T(8,128)(2,1)} %convolution_convert_fusion.7.x_ref), custom_call_target="tpu_custom_call" | custom-call | tf_op jit(solution)/shard_map/tensor_sum/pallas_call | solution.py:160
  110.6 28.8 %tensor_sum.17 = bf16[256,1152]{1,0:T(8,128)(2,1)} custom-call(bf16[256,1152]{1,0:T(8,128)(2,1)} %fusion.44.x_ref), custom_call_target="tpu_custom_call" | custom-call | tf_op jit(solution)/shard_map/tensor_sum/pallas_call | solution.py:160
  146.1 7.3 collective-permute-done
  158.5 15.2 %all-gather.8.cloned.1.call-done = bf16[1,1024,576]{1,2,0:T(8,128)(2,1)} async-done(((bf16[1,256,576]{1,2,0:T(8,128)(2,1)}), bf16[1,1024,576]{1,2,0:T(8,128)(2,1)}) %all-gather.8.cloned.1.call-update) | async-done | bytes 1179664 | tf_op jit(solution)/shard_map/all_gather | solution.py:344
  181.0 31.5 %tensor_sum.18 = bf16[256,1152]{1,0:T(8,128)(2,1)} custom-call(bf16[256,1152]{1,0:T(8,128)(2,1)} %convolution_convert_fusion.6.x_ref), custom_call_target="tpu_custom_call" | custom-call | tf_op jit(solution)/shard_map/tensor_sum/pallas_call | solution.py:160
  219.8 28.7 %tensor_sum.19 = bf16[256,1152]{1,0:T(8,128)(2,1)} custom-call(bf16[256,1152]{1,0:T(8,128)(2,1)} %fusion.47.x_ref), custom_call_target="tpu_custom_call" | custom-call | tf_op jit(solution)/shard_map/tensor_sum/pallas_call | solution.py:160
  268.2 15.2 %all-gather.10.cloned.1.call-done = bf16[1,1024,576]{1,2,0:T(8,128)(2,1)} async-done(((bf16[1,256,576]{1,2,0:T(8,128)(2,1)}), bf16[1,1024,576]{1,2,0:T(8,128)(2,1)}) %all-gather.10.cloned.1.call-update) | async-done | bytes 1179664 | tf_op jit(solution)/shard_map/all_gather | solution.py:344
  290.6 31.5 %tensor_sum.20 = bf16[256,1152]{1,0:T(8,128)(2,1)} custom-call(bf16[256,1152]{1,0:T(8,128)(2,1)} %convolution_convert_fusion.5.x_ref), custom_call_target="tpu_custom_call" | custom-call | tf_op jit(solution)/shard_map/tensor_sum/pallas_call | solution.py:160
  329.5 28.6 %tensor_sum.21 = bf16[256,1152]{1,0:T(8,128)(2,1)} custom-call(bf16[256,1152]{1,0:T(8,128)(2,1)} %fusion.50.x_ref), custom_call_target="tpu_custom_call" | custom-call | tf_op jit(solution)/shard_map/tensor_sum/pallas_call | solution.py:160
  377.8 15.2 %all-gather.12.cloned.1.call-done = bf16[1,1024,576]{1,2,0:T(8,128)(2,1)} async-done(((bf16[1,256,576]{1,2,0:T(8,128)(2,1)}), bf16[1,1024,576]{1,2,0:T(8,128)(2,1)}) %all-gather.12.cloned.1.call-update) | async-done | bytes 1179664 | tf_op jit(solution)/shard_map/all_gather | solution.py:344
  400.2 31.5 %tensor_sum.22 = bf16[256,1152]{1,0:T(8,128)(2,1)} custom-call(bf16[256,1152]{1,0:T(8,128)(2,1)} %convolution_convert_fusion.4.x_ref), custom_call_target="tpu_custom_call" | custom-call | tf_op jit(solution)/shard_map/tensor_sum/pallas_call | solution.py:160
  442.0 28.8 %tensor_sum.24 = bf16[256,1152]{1,0:T(8,128)(2,1)} custom-call(bf16[256,1152]{1,0:T(8,128)(2,1)} %fusion.32.x_ref), custom_call_target="tpu_custom_call" | custom-call | tf_op jit(solution)/shard_map/tensor_sum/pallas_call | solution.py:160
  494.4 17.3 %owner_sum.4 = f32[256,576]{1,0:T(8,128)} custom-call(bf16[1024,576]{1,0:T(8,128)(2,1)} %pad_maximum_fusion.x_ref), custom_call_target="tpu_custom_call" | custom-call | tf_op jit(solution)/shard_map/owner_sum/pallas_call | solution.py:208
  516.9 29.5 %tensor_sum.25 = bf16[256,1152]{1,0:T(8,128)(2,1)} custom-call(bf16[256,1152]{1,0:T(8,128)(2,1)} %fusion.56.x_ref), custom_call_target="tpu_custom_call" | custom-call | tf_op jit(solution)/shard_map/tensor_sum/pallas_call | solution.py:160
  554.9 13.2 %collective-permute-done.3 = bf16[1,256,1152]{2,1,0:T(8,128)(2,1)S(1)} collective-permute-done((bf16[1,256,1152]{2,1,0:T(8,128)(2,1)S(1)}, bf16[1,256,1152]{2,1,0:T(8,128)(2,1)S(1)}, u32[]{:S(2)}, u32[]{:S(2)}) %collective-permute-start.3) | collective-permute-done | bytes 589856 | tf_op jit(solution)/shard_map/ppermute | solution.py:222
  574.1 29.6 %tensor_sum.26 = bf16[256,1152]{1,0:T(8,128)(2,1)} custom-call(bf16[256,1152]{1,0:T(8,128)(2,1)} %fusion.35.x_ref), custom_call_target="tpu_custom_call" | custom-call | tf_op jit(solution)/shard_map/tensor_sum/pallas_call | solution.py:160
  628.9 17.1 %owner_sum.5 = f32[256,576]{1,0:T(8,128)} custom-call(bf16[1024,576]{1,0:T(8,128)(2,1)} %pad_maximum_fusion.1.x_ref), custom_call_target="tpu_custom_call" | custom-call | tf_op jit(solution)/shard_map/owner_sum/pallas_call | solution.py:208
  651.4 29.7 %tensor_sum.27 = bf16[256,1152]{1,0:T(8,128)(2,1)} custom-call(bf16[256,1152]{1,0:T(8,128)(2,1)} %fusion.57.x_ref), custom_call_target="tpu_custom_call" | custom-call | tf_op jit(solution)/shard_map/tensor_sum/pallas_call | solution.py:160
  689.5 13.9 %collective-permute-done.4 = bf16[1,256,1152]{2,1,0:T(8,128)(2,1)S(1)} collective-permute-done((bf16[1,256,1152]{2,1,0:T(8,128)(2,1)S(1)}, bf16[1,256,1152]{2,1,0:T(8,128)(2,1)S(1)}, u32[]{:S(2)}, u32[]{:S(2)}) %collective-permute-start.4) | collective-permute-done | bytes 589856 | tf_op jit(solution)/shard_map/ppermute | solution.py:222
  709.3 29.2 %tensor_sum.28 = bf16[256,1152]{1,0:T(8,128)(2,1)} custom-call(bf16[256,1152]{1,0:T(8,128)(2,1)} %fusion.38.x_ref), custom_call_target="tpu_custom_call" | custom-call | tf_op jit(solution)/shard_map/tensor_sum/pallas_call | solution.py:160
  764.5 17.2 %owner_sum.6 = f32[256,576]{1,0:T(8,128)} custom-call(bf16[1024,576]{1,0:T(8,128)(2,1)} %pad_maximum_fusion.2.x_ref), custom_call_target="tpu_custom_call" | custom-call | tf_op jit(solution)/shard_map/owner_sum/pallas_call | solution.py:208
  786.9 29.5 %tensor_sum.29 = bf16[256,1152]{1,0:T(8,128)(2,1)} custom-call(bf16[256,1152]{1,0:T(8,128)(2,1)} %fusion.58.x_ref), custom_call_target="tpu_custom_call" | custom-call | tf_op jit(solution)/shard_map/tensor_sum/pallas_call | solution.py:160
  849.9 29.3 %tensor_sum.30 = bf16[256,1152]{1,0:T(8,128)(2,1)} custom-call(bf16[256,1152]{1,0:T(8,128)(2,1)} %fusion.41.x_ref), custom_call_target="tpu_custom_call" | custom-call | tf_op jit(solution)/shard_map/tensor_sum/pallas_call | solution.py:160
  908.0 23.2 %owner_sum.7 = f32[256,576]{1,0:T(8,128)} custom-call(bf16[1024,576]{1,0:T(8,128)(2,1)} %pad_maximum_fusion.3.x_ref), custom_call_target="tpu_custom_call" | custom-call | tf_op jit(solution)/shard_map/owner_sum/pallas_call | solution.py:208
  942.6 29.7 %tensor_sum.31 = bf16[256,1152]{1,0:T(8,128)(2,1)} custom-call(bf16[256,1152]{1,0:T(8,128)(2,1)} %fusion.59.x_ref), custom_call_target="tpu_custom_call" | custom-call | tf_op jit(solution)/shard_map/tensor_sum/pallas_call | solution.py:160
  983.9 7.1 convolution_convert_fusion
  996.3 28.5 %tensor_sum.23 = bf16[256,1152]{1,0:T(8,128)(2,1)} custom-call(bf16[256,1152]{1,0:T(8,128)(2,1)} %fusion.53.x_ref), custom_call_target="tpu_custom_call" | custom-call | tf_op jit(solution)/shard_map/tensor_sum/pallas_call | solution.py:160
  1064.1 11.1 all-reduce
  1077.6 23.2 %psum.51 = f32[3,288]{1,0:T(4,128)S(1)} all-reduce(f32[3,288]{1,0:T(4,128)S(1)} %fusion.307), channel_id=1, replica_groups=mesh['section'=2,'tensor'=4,'ctx'=4] {'section','tensor'}, use_global_device_ids=true, to_apply=%region_70.71 | all-reduce | flops 864 | bytes 6912 | tf_op jit(solution)/shard_map/psum | solution.py:607
  (887 shorter events, 389.7 us)
Async XLA Ops:
  7.2 98.7 %copy-start = (bf16[1,1152,1152]{2,1,0:T(8,128)(2,1)S(1)}, bf16[1,1152,1152]{2,1,0:T(8,128)(2,1)}, u32[]{:S(2)}) copy-start(bf16[1,1152,1152]{2,1,0:T(8,128)(2,1)} %param.22) | copy-start | bytes 7962628
  7.2 55.2 %all-gather.6.cloned.1.call-start = ((), (), s32[]{:S(2)}) async-start(), calls=%async_computation.4 | async-start | bytes 1474560 | tf_op jit(solution)/shard_map/all_gather | solution.py:344
  8.9 30.3 %copy-start.264 = (f32[1,2,288]{2,1,0:T(2,128)S(1)}, f32[1,2,288]{2,1,0:T(2,128)}, u32[]{:S(2)}) copy-start(f32[1,2,288]{2,1,0:T(2,128)} %param.19) | copy-start | bytes 6916
  44.6 129.1 %all-gather.8.cloned.1.call-start = ((), (), s32[]{:S(2)}) async-start(), calls=%async_computation.5 | async-start | bytes 1474560 | tf_op jit(solution)/shard_map/all_gather | solution.py:344
  45.7 18.0 %copy-start.154 = (f32[4,72]{1,0:T(4,128)}, f32[4,72]{1,0:T(4,128)S(1)}, u32[]{:S(2)}) copy-start(f32[4,72]{1,0:T(4,128)S(1)} %add.639) | copy-start | bytes 3460
  142.4 11.0 collective-permute-start
  153.7 94.8 %copy-start.9 = (bf16[1,256,1152]{2,1,0:T(8,128)(2,1)}, bf16[1,256,1152]{2,1,0:T(8,128)(2,1)S(1)}, u32[]{:S(2)}) copy-start(bf16[1,256,1152]{2,1,0:T(8,128)(2,1)S(1)} %get-tuple-element.125) | copy-start | bytes 1769476
  156.8 126.6 %all-gather.10.cloned.1.call-start = ((), (), s32[]{:S(2)}) async-start(), calls=%async_computation.6 | async-start | bytes 1474560 | tf_op jit(solution)/shard_map/all_gather | solution.py:344
  251.3 10.8 collective-permute-start.1
  263.4 94.7 %copy-start.12 = (bf16[1,256,1152]{2,1,0:T(8,128)(2,1)}, bf16[1,256,1152]{2,1,0:T(8,128)(2,1)S(1)}, u32[]{:S(2)}) copy-start(bf16[1,256,1152]{2,1,0:T(8,128)(2,1)S(1)} %get-tuple-element.121) | copy-start | bytes 1769476
  266.4 126.6 %all-gather.12.cloned.1.call-start = ((), (), s32[]{:S(2)}) async-start(), calls=%async_computation.7 | async-start | bytes 1474560 | tf_op jit(solution)/shard_map/all_gather | solution.py:344
  360.9 10.9 collective-permute-start.2
  376.1 730.2 %reduce-scatter.13.cloned.1.call-start = ((), (), s32[]{:S(2)}) async-start(), calls=%async_computation.11 | async-start | bytes 1105920
  553.2 14.9 %collective-permute-start.3 = (bf16[1,256,1152]{2,1,0:T(8,128)(2,1)S(1)}, bf16[1,256,1152]{2,1,0:T(8,128)(2,1)S(1)}, u32[]{:S(2)}, u32[]{:S(2)}) collective-permute-start(bf16[1,256,1152]{2,1,0:T(8,128)(2,1)S(1)} %get-tuple-element.114), channel_id=1, source_target_pairs={{16,0},{17,1},{18,2},{19,3},{20,4},{21,5},{22,6},{23,7},{24,8},{25... | collective-permute-start | bytes 1769480 | tf_op jit(solution)/shard_map/ppermute | solution.py:222
  688.2 15.2 %collective-permute-start.4 = (bf16[1,256,1152]{2,1,0:T(8,128)(2,1)S(1)}, bf16[1,256,1152]{2,1,0:T(8,128)(2,1)S(1)}, u32[]{:S(2)}, u32[]{:S(2)}) collective-permute-start(bf16[1,256,1152]{2,1,0:T(8,128)(2,1)S(1)} %get-tuple-element.112), channel_id=1, source_target_pairs={{16,0},{17,1},{18,2},{19,3},{20,4},{21,5},{22,6},{23,7},{24,8},{25... | collective-permute-start | bytes 1769480 | tf_op jit(solution)/shard_map/ppermute | solution.py:222
  823.6 19.3 %collective-permute-start.5 = (bf16[1,256,1152]{2,1,0:T(8,128)(2,1)}, bf16[1,256,1152]{2,1,0:T(8,128)(2,1)}, u32[]{:S(2)}, u32[]{:S(2)}) collective-permute-start(bf16[1,256,1152]{2,1,0:T(8,128)(2,1)} %get-tuple-element.110), channel_id=1, source_target_pairs={{16,0},{17,1},{18,2},{19,3},{20,4},{21,5},{22,6},{23,7},{24,8},{25... | collective-permute-start | bytes 1769480 | tf_op jit(solution)/shard_map/ppermute | solution.py:222
  900.5 207.6 %reduce-scatter.7.cloned.1.call-start = ((), (), s32[]{:S(2)}) async-start(), calls=%async_computation.8 | async-start | bytes 3317760 | tf_op jit(solution)/shard_map/reduce_scatter | solution.py:586
  908.0 25.3 %copy-start.100 = (bf16[1,256,4,72]{1,3,2,0:T(8,128)(2,1)S(1)}, bf16[1,256,4,72]{1,3,2,0:T(8,128)(2,1)}, u32[]{:S(2)}) copy-start(bf16[1,256,4,72]{1,3,2,0:T(8,128)(2,1)} %get-tuple-element.167) | copy-start | bytes 442372
  942.6 29.7 %copy-start.136 = (f32[1152]{0:T(1024)S(1)}, f32[1152]{0:T(1024)}, u32[]{:S(2)}) copy-start(f32[1152]{0:T(1024)} %copy-done.135) | copy-start | bytes 13828
  942.6 29.7 %copy-start.187 = (f32[1152]{0:T(1024)S(1)}, f32[1152]{0:T(1024)}, u32[]{:S(2)}) copy-start(f32[1152]{0:T(1024)} %copy-done.186) | copy-start | bytes 13828
  942.6 29.8 %copy-start.224 = (f32[256]{0:T(256)S(1)}, f32[256]{0:T(256)}, u32[]{:S(2)}) copy-start(f32[256]{0:T(256)} %copy-done.223) | copy-start | bytes 3076
  942.6 29.8 %copy-start.240 = (f32[256]{0:T(256)S(1)}, f32[256]{0:T(256)}, u32[]{:S(2)}) copy-start(f32[256]{0:T(256)} %copy-done.239) | copy-start | bytes 3076
  983.8 126.5 %reduce-scatter.11.cloned.1.call-start = ((), (), s32[]{:S(2)}) async-start(), calls=%async_computation.10 | async-start | bytes 3317760 | tf_op jit(solution)/shard_map/reduce_scatter | solution.py:595
  991.0 121.6 %reduce-scatter.9.cloned.1.call-start = ((), (), s32[]{:S(2)}) async-start(), calls=%async_computation.9 | async-start | bytes 3317760 | tf_op jit(solution)/shard_map/reduce_scatter | solution.py:592
  996.2 28.5 %copy-start.247 = (f32[4,72]{1,0:T(4,128)S(1)}, f32[4,72]{1,0:T(4,128)}, u32[]{:S(2)}) copy-start(f32[4,72]{1,0:T(4,128)} %get-tuple-element.160) | copy-start | bytes 3460
  996.3 29.8 %copy-start.197 = (f32[1152]{0:T(1024)S(1)}, f32[1152]{0:T(1024)}, u32[]{:S(2)}) copy-start(f32[1152]{0:T(1024)} %get-tuple-element.63) | copy-start | bytes 13828
  996.3 29.8 %copy-start.199 = (f32[1152]{0:T(1024)S(1)}, f32[1152]{0:T(1024)}, u32[]{:S(2)}) copy-start(f32[1152]{0:T(1024)} %get-tuple-element.39) | copy-start | bytes 13828
  996.3 29.8 %copy-start.195 = (f32[1152]{0:T(1024)S(1)}, f32[1152]{0:T(1024)}, u32[]{:S(2)}) copy-start(f32[1152]{0:T(1024)} %get-tuple-element.27) | copy-start | bytes 13828
  996.3 29.8 %copy-start.196 = (f32[1152]{0:T(1024)S(1)}, f32[1152]{0:T(1024)}, u32[]{:S(2)}) copy-start(f32[1152]{0:T(1024)} %get-tuple-element.61) | copy-start | bytes 13828
  1061.0 39.8 %copy-start.181 = (f32[3,288]{1,0:T(4,128)S(1)}, f32[3,288]{1,0:T(4,128)}, u32[]{:S(2)}) copy-start(f32[3,288]{1,0:T(4,128)} %param.14) | copy-start | bytes 10372
  1077.6 25.1 %copy-start.263 = (f32[256]{0:T(256)S(1)}, f32[256]{0:T(256)}, u32[]{:S(2)}) copy-start(f32[256]{0:T(256)} %get-tuple-element.52) | copy-start | bytes 3076
  1077.6 25.1 %copy-start.262 = (f32[256]{0:T(256)S(1)}, f32[256]{0:T(256)}, u32[]{:S(2)}) copy-start(f32[256]{0:T(256)} %get-tuple-element.16) | copy-start | bytes 3076
  (263 other events, 871.8 us)
Sparse Core Ops, SparseCore 0:
  44.7 17.6 all-gather.5
  156.9 16.7 all-gather.7
  266.5 16.7 all-gather.9
  376.2 16.7 all-gather.11
  900.6 29.5 reduce-scatter.12
  984.0 35.1 reduce-scatter.6
  1021.7 34.7 reduce-scatter.10
  1059.0 34.6 reduce-scatter.8
